TPU v7x, 32 devices: a whole 2x2x4 slice. The times are simulated.
32 devices in a mesh: shot: 4 (over y, x), blk: 8 (over z, core).
Axes of the slice: x: 2, y: 2, z: 4, core: 2. Of those that a mesh axis runs over, the one named last changes fastest.
Arguments:
- intensities: bfloat16 [2048, 16, 128], P('blk', 'shot'), may hold values from -6 to 6
- tile_owner: int32 [2048], P('blk'), may hold values from 0 to 7, as said below
- tile_place: int32 [2048], P('blk'), may hold values from 0 to 255
- tile_kernel: int32 [2048], P('blk'), may hold values from 0 to 3
- mask_len: int32 [2048], P('blk'), may hold values from 1 to 128
- interp_weights: bfloat16 [4, 128, 128], replicated, may hold values from 0 to 1.2
Outputs:
- corr_diff: float32 [16, 128, 2048], P('shot', 'blk')
Inputs may be any that keep to these rules, and one draw needn't show every extreme that they name: `tile_owner`: in each device's block of 256 tiles no owner is named by more than 96 tiles, and one owner, the same for every block, is named by exactly 96 tiles of every block.
All inputs are finite; a program needn't handle non-finite values.
Results may differ from a plain program's by a relative error of at most 0.0003.
Values may be sent and summed in bfloat16 or wider, within the bound.
No kernel may reach another device: no remote copies, remote signals or barrier semaphores. Data moves between devices by JAX's collectives and lax.ppermute only.
A program may use at most 64 MiB of HBM per device.

v0:
```python
import math

import jax
import jax.numpy as jnp
import ml_dtypes
import numpy as np
from jax import lax
from jax.experimental import pallas as pl
from jax.experimental.pallas import tpu as pltpu
from jax.sharding import PartitionSpec as P


ANG = 2048
TP = 128
Q_DEV = 16
NSEG = 16
HALF = NSEG // 2 + 1
SLOTS = Q_DEV * NSEG
LANES = 128
META = 8
TWIST = 2 * 2 * TP
ROOT = math.sqrt(0.5)
COS1, SIN1 = math.cos(math.pi / 8), math.sin(math.pi / 8)


F32 = jnp.float32
BF16 = jnp.bfloat16


def pieces(array, count):
    terms = []
    for _ in range(count):
        terms.append(array.astype(np.float32).astype(ml_dtypes.bfloat16))
        array = array - terms[-1].astype(np.float64)
    return terms


def dft_table():
    lane = np.arange(TP)
    angle = 2.0 * np.pi * (np.outer(lane, lane) % TP) / TP
    cosine, sine = np.cos(angle), np.sin(angle)
    factors = np.block([[cosine, sine], [-sine, cosine]])
    turn = 2.0 * np.pi * np.outer(np.arange(NSEG), lane) / ANG
    twist = np.concatenate([np.cos(turn), np.sin(turn)], axis=1)
    return np.concatenate(pieces(factors, 2) + pieces(twist, 3), axis=0)


def split(value):
    high = value.astype(BF16)
    return high, (value - high.astype(F32)).astype(BF16)


def dot(a, b):
    return jnp.dot(a, b, preferred_element_type=F32)


def dot_rows(a, b):
    return lax.dot_general(a, b, (((1,), (1,)), ((), ())), preferred_element_type=F32)


def iota(shape, axis):
    return lax.broadcasted_iota(jnp.int32, shape, axis)


def factor_dot(value, table_ref):
    high, low = split(value)
    table_high, table_low = table_ref[: 2 * TP, :], table_ref[2 * TP : TWIST, :]
    return dot(high, table_high) + (dot(high, table_low) + dot(low, table_high))


def twist_of(table_ref):
    terms = [
        table_ref[TWIST + i * NSEG : TWIST + (i + 1) * NSEG, :].astype(F32) for i in range(3)
    ]
    whole = terms[0] + (terms[1] + terms[2])
    return [(whole[k : k + 1, :TP], whole[k : k + 1, TP:]) for k in range(HALF)]


def real_dft(x):
    a = [x[j] + x[j + 8] for j in range(8)]
    b = [x[j] - x[j + 8] for j in range(8)]
    c = [None] + [b[j] - b[8 - j] for j in range(1, 4)]
    s = [None] + [b[j] + b[8 - j] for j in range(1, 4)]
    a2 = [a[j] + a[j + 4] for j in range(4)]
    b2 = [a[j] - a[j + 4] for j in range(4)]
    real, imag = [None] * 9, [None] * 9
    even, odd = a2[0] + a2[2], a2[1] + a2[3]
    real[0], real[8] = even + odd, even - odd
    real[4], imag[4] = a2[0] - a2[2], a2[1] - a2[3]
    left, right = ROOT * (b2[1] - b2[3]), ROOT * (b2[1] + b2[3])
    real[2], real[6] = b2[0] + left, b2[0] - left
    imag[2], imag[6] = right + b2[2], right - b2[2]
    side, rise = ROOT * c[2], ROOT * s[2]
    for k, even, odd, odd_sine, even_sine in (
        (1, b[0] + side, COS1 * c[1] + SIN1 * c[3], SIN1 * s[1] + COS1 * s[3], rise + b[4]),
        (3, b[0] - side, SIN1 * c[1] - COS1 * c[3], COS1 * s[1] - SIN1 * s[3], rise - b[4]),
    ):
        real[k], real[8 - k] = even + odd, even - odd
        imag[k], imag[8 - k] = odd_sine + even_sine, odd_sine - even_sine
    return real, imag


def real_inverse(p, n):
    u1, v1, u3, v3 = p[1] + p[7], p[1] - p[7], p[3] + p[5], p[3] - p[5]
    x1, y1, x3, y3 = n[1] + n[7], n[1] - n[7], n[3] + n[5], n[3] - n[5]
    a = [u1 + u3, COS1 * v1 + SIN1 * v3, ROOT * (u1 - u3), SIN1 * v1 - COS1 * v3]
    b = [None, SIN1 * x1 + COS1 * x3, ROOT * (y1 + y3), COS1 * x1 - SIN1 * x3, y1 - y3]
    odd = [a[0], a[1] - b[1], a[2] - b[2], a[3] - b[3], -b[4]]
    odd += [-a[3] - b[3], -a[2] - b[2], -a[1] - b[1]]
    zero, eight = 0.5 * p[0], 0.5 * p[8]
    e0, e1 = zero + eight, zero - eight
    c, d = p[2] + p[6], ROOT * (p[2] - p[6])
    e, f = ROOT * (n[2] + n[6]), n[2] - n[6]
    up, down = e0 + p[4], e0 - p[4]
    left, right = e1 - n[4], e1 + n[4]
    near, far = d - e, d + e
    even = [up + c, left + near, down - f, right - far, up - c, left - near, down + f, right + far]
    return [even[m] + odd[m] for m in range(8)] + [even[m] - odd[m] for m in range(8)]


def slabs(value, count):
    return [value[k * Q_DEV : (k + 1) * Q_DEV, :] for k in range(count)]


def spectrum(cycles, table_ref):
    twist = twist_of(table_ref)
    reals, imags = [], []
    for cycle in cycles:
        real, imag = real_dft(slabs(cycle, NSEG))
        for k, (cosine, sine) in enumerate(twist):
            if k == 0:
                reals.append(real[k])
                imags.append(jnp.zeros_like(real[k]))
            elif imag[k] is None:
                reals.append(real[k] * cosine)
                imags.append(real[k] * sine)
            else:
                reals.append(real[k] * cosine - imag[k] * sine)
                imags.append(imag[k] * cosine + real[k] * sine)
    grid = jnp.concatenate(
        [jnp.concatenate(reals, axis=0), jnp.concatenate(imags, axis=0)], axis=1
    )
    return factor_dot(grid, table_ref)


def correlation(grid, twist):
    real, imag = slabs(grid[:, :TP], HALF), slabs(grid[:, TP:], HALF)
    p, n = [real[0]], [None]
    for k in range(1, HALF):
        cosine, sine = twist[k]
        p.append(real[k] * cosine - imag[k] * sine)
        n.append(None if k == HALF - 1 else real[k] * sine + imag[k] * cosine)
    return real_inverse(p, n)


def pack_kernel(owners, capacity, me_ref, owner_hbm, place_hbm, kern_hbm, len_hbm, pix_hbm, *rest):
    chips = owners // 2
    first, later = rest[:chips], rest[chips : 2 * chips]
    swap_first, swap_later, ints, pix, wide, sems = rest[2 * chips :]
    tiles = ints.shape[1]
    shots = pix.shape[0] // tiles
    first_rows, later_rows = capacity + META, (shots - 1) * capacity
    copies = [
        pltpu.make_async_copy(source, ints.at[pl.ds(8 * i, 1), :], sems.at[i])
        for i, source in enumerate((owner_hbm, place_hbm, kern_hbm, len_hbm))
    ]
    copies.append(pltpu.make_async_copy(pix_hbm, pix, sems.at[4]))
    for copy in copies:
        copy.start()
    before = (iota((tiles, tiles), 0) < iota((tiles, tiles), 1)).astype(F32).astype(BF16)
    for copy in copies[:4]:
        copy.wait()
    owner = ints[0:1, :]
    mine = (iota((owners, tiles), 0) == owner).astype(F32)
    rank = jnp.sum(dot(mine.astype(BF16), before) * mine, axis=0, keepdims=True)
    slot = (owner ^ me_ref[0]) * LANES + rank.astype(jnp.int32)
    place = ints[8:9, :]
    meta = jnp.concatenate(
        [
            ((place % NSEG) * Q_DEV + place // NSEG).astype(F32),
            (ints[16:17, :] + 1).astype(F32),
            ints[24:25, :].astype(F32),
            jnp.zeros((META - 3, tiles), F32),
        ],
        axis=0,
    ).astype(BF16)
    placing = [
        (iota((LANES, tiles), 0) + d * LANES == slot).astype(F32).astype(BF16)
        for d in range(owners)
    ]
    tags = [dot_rows(meta, placing[d]).astype(BF16) for d in range(owners)]
    copies[4].wait()
    wide[...] = pix[...].astype(F32)
    pixels = jnp.concatenate(
        [wide[pl.ds(s, tiles, stride=shots), :].astype(BF16) for s in range(shots)], axis=1
    )
    for d in range(owners):
        sent = dot(placing[d][:capacity], pixels).astype(BF16)
        j = d // 2
        if d % 2:
            near, far, at, to = swap_first, swap_later, j * first_rows, j * later_rows
        else:
            near, far, at, to = first[j], later[j], 0, 0
        near[at : at + capacity, :] = sent[:, :TP]
        near[at + capacity : at + first_rows, :] = tags[d]
        for s in range(1, shots):
            start = to + (s - 1) * capacity
            far[start : start + capacity, :] = sent[:, s * TP : (s + 1) * TP]


def merge_kernel(chips, *refs):
    own, other, outs = refs[: chips - 1], refs[chips - 1], refs[chips:]
    rows = own[0].shape[0]
    for j in range(1, chips):
        outs[j - 1][:rows, :] = own[j - 1][...]
        outs[j - 1][rows:, :] = other[j * rows : (j + 1) * rows, :]


def sources(own, other, far, rows):
    blocks = [own, other.at[pl.ds(0, rows), :]]
    for ref in far:
        blocks += [ref.at[pl.ds(0, rows), :], ref.at[pl.ds(rows, rows), :]]
    return blocks


def weigh(sums, count, weights_ref):
    kernels = weights_ref.shape[0]
    weights = weights_ref[...].reshape(kernels * TP, TP)
    cycles = []
    for s in range(count):
        columns = slice(s * TP, (s + 1) * TP)
        high, low = split(
            jnp.concatenate(
                [sums[k * SLOTS : (k + 1) * SLOTS, columns] for k in range(kernels)], axis=1
            )
        )
        cycles.append(dot(high, weights) + dot(low, weights))
    return cycles


def gather_kernel(owners, capacity, *refs):
    weights_hbm, pick_ref, live_ref, cyc0_ref, mask_ref, table, weights_ref, sem = refs[-8:]
    copy = pltpu.make_async_copy(weights_hbm, weights_ref, sem)
    copy.start()
    got = sources(refs[0], refs[1], refs[2:-8], capacity + META)
    kernels = weights_ref.shape[0]
    metas = [g[capacity : capacity + META, :].astype(F32) for g in got]
    group = math.gcd(owners, 8)
    for base in range(0, owners, group):
        lens = jnp.concatenate([m[2:3] for m in metas[base : base + group]], axis=0)
        lens = jnp.transpose(lens)
        for i in range(group):
            d = base + i
            rows = slice(d * capacity, (d + 1) * capacity)
            live = iota((capacity, TP), 1).astype(F32) < lens[:capacity, i : i + 1]
            live = jnp.where(live, 1.0, 0.0).astype(BF16)
            live_ref[rows, :] = live
            table[rows, :TP] = got[d][:capacity, :] * live
            table[rows, TP:] = live
    index = [
        jnp.where(m[1:2] > 0.5, m[0:1] + (m[1:2] - 1.0) * SLOTS, -1.0)[:, :capacity] for m in metas
    ]
    index = jnp.concatenate(index, axis=1).astype(jnp.int32)
    hit = iota((kernels * SLOTS, owners * capacity), 0) == index
    pick = hit.astype(F32).astype(BF16)
    pick_ref[...] = pick
    sums = dot(pick, table[...])
    copy.wait()
    cyc0_ref[...], mask_ref[...] = weigh(sums, 2, weights_ref)


def scale_kernel(cyc0_ref, mask_ref, table_ref, spec_ref, scale_ref):
    spec = spectrum([cyc0_ref[...], mask_ref[...]], table_ref)
    rows = spec_ref.shape[0]
    spec_ref[...] = spec[:rows]
    real, imag = spec[rows:, :TP], spec[rows:, TP:]
    power = jnp.concatenate([real * real + imag * imag, jnp.zeros_like(real)], axis=1)
    corr = correlation(factor_dot(power, table_ref), twist_of(table_ref))
    least = jnp.maximum(corr[0][:, :1] * (0.01 * 2.0 / ANG), 1.0)
    for m in range(NSEG):
        whole = jnp.maximum(corr[m] * (2.0 / ANG), least)
        scale_ref[m * Q_DEV : (m + 1) * Q_DEV, :] = (2.0 / ANG) / whole


def correlate_kernel(owners, capacity, *refs):
    (weights_ref, pick_ref, live_ref, spec_ref, next_ref, scale_ref, table_ref, out_hbm, table,
     out, sems) = refs[-11:]
    shots = out.shape[0]
    got = sources(refs[0], refs[1], refs[2:-11], (shots - 1) * capacity)
    for d in range(owners):
        rows = slice(d * capacity, (d + 1) * capacity)
        live = live_ref[rows, :]
        for s in range(shots - 1):
            table[rows, s * TP : (s + 1) * TP] = (
                got[d][s * capacity : (s + 1) * capacity, :] * live
            )
    cycles = weigh(dot(pick_ref[...], table[...]), shots - 1, weights_ref)
    spec = jnp.concatenate([spec_ref[...], spectrum(cycles + [next_ref[...]], table_ref)], axis=0)
    rows = HALF * Q_DEV
    diff = spec[: shots * rows] - spec[rows:]
    spec = spec[: shots * rows]
    real, imag = spec[:, :TP], spec[:, TP:]
    diff_real, diff_imag = diff[:, :TP], diff[:, TP:]
    cross = jnp.concatenate(
        [real * diff_real + imag * diff_imag, real * diff_imag - imag * diff_real], axis=1
    )
    grid = factor_dot(cross, table_ref)
    twist = twist_of(table_ref)
    copies = []
    for s in range(shots):
        corr = correlation(grid[s * rows : (s + 1) * rows], twist)
        for m in range(NSEG):
            out[s, :, m * TP : (m + 1) * TP] = corr[m] * scale_ref[m * Q_DEV : (m + 1) * Q_DEV, :]
        copies.append(pltpu.make_async_copy(out.at[s], out_hbm.at[s], sems.at[s]))
        copies[-1].start()
    for copy in copies:
        copy.wait()


VMEM = pl.BlockSpec(memory_space=pltpu.VMEM)
SMEM = pl.BlockSpec(memory_space=pltpu.SMEM)
HBM = pl.BlockSpec(memory_space=pltpu.HBM)


def call(body, outs, operands, in_specs=None, out_specs=None, scratch=(), flops=0, limit=20 << 20):
    return pl.pallas_call(
        body,
        out_shape=outs,
        in_specs=in_specs or [VMEM] * len(operands),
        out_specs=out_specs or jax.tree.map(lambda _: VMEM, outs),
        scratch_shapes=list(scratch),
        compiler_params=pltpu.CompilerParams(vmem_limit_bytes=limit),
        cost_estimate=pl.CostEstimate(flops=flops, bytes_accessed=1 << 20, transcendentals=0),
    )(*operands)


def far_order(owners):
    return sorted(range(2, owners, 2), key=lambda d: (d < owners // 2, -d))


def cross(block, d, owners):
    return lax.ppermute(block, "blk", [(i, i ^ d) for i in range(owners)])


def exchange(own, swap, owners):
    chips = owners // 2
    other = cross(swap, 1, owners)
    rows = own[0].shape[0]
    merged = call(
        lambda *refs: merge_kernel(chips, *refs),
        [jax.ShapeDtypeStruct((2 * rows, TP), BF16)] * (chips - 1),
        [*own[1:], other],
    )
    far = {d: cross(merged[d // 2 - 1], d, owners) for d in far_order(owners)}
    return [own[0], other] + [far[d] for d in range(2, owners, 2)]


def program(intensities, tile_owner, tile_place, tile_kernel, mask_len, interp_weights):
    owners = lax.axis_size("blk")
    chips = owners // 2
    ring = lax.axis_size("shot")
    tiles, shots, _ = intensities.shape
    kernels = interp_weights.shape[0]
    capacity = -(-(3 * tiles // owners) // 16) * 16
    rows = owners * capacity
    table = jnp.asarray(dft_table())
    me = lax.axis_index("blk").astype(jnp.int32).reshape(1)
    sent = call(
        lambda *refs: pack_kernel(owners, capacity, *refs),
        [jax.ShapeDtypeStruct((capacity + META, TP), BF16)] * chips
        + [jax.ShapeDtypeStruct(((shots - 1) * capacity, TP), BF16)] * chips
        + [jax.ShapeDtypeStruct((chips * (capacity + META), TP), BF16)]
        + [jax.ShapeDtypeStruct((chips * (shots - 1) * capacity, TP), BF16)],
        [
            me,
            *(
                pltpu.with_memory_space_constraint(v, pltpu.HBM)
                for v in (
                    tile_owner.reshape(1, tiles),
                    tile_place.reshape(1, tiles),
                    tile_kernel.reshape(1, tiles),
                    mask_len.reshape(1, tiles),
                    intensities.reshape(tiles * shots, TP),
                )
            ),
        ],
        in_specs=[SMEM] + [HBM] * 5,
        scratch=[
            pltpu.VMEM((32, tiles), jnp.int32),
            pltpu.VMEM((tiles * shots, TP), BF16),
            pltpu.VMEM((tiles * shots, TP), F32),
            pltpu.SemaphoreType.DMA((5,)),
        ],
    )
    early = exchange(sent[:chips], sent[2 * chips], owners)
    late = exchange(sent[chips : 2 * chips], sent[2 * chips + 1], owners)
    pick, live, cyc0, mask = call(
        lambda *refs: gather_kernel(owners, capacity, *refs),
        [
            jax.ShapeDtypeStruct((kernels * SLOTS, rows), BF16),
            jax.ShapeDtypeStruct((rows, TP), BF16),
            jax.ShapeDtypeStruct((SLOTS, TP), F32),
            jax.ShapeDtypeStruct((SLOTS, TP), F32),
        ],
        [*early, pltpu.with_memory_space_constraint(interp_weights, pltpu.HBM)],
        in_specs=[VMEM] * len(early) + [HBM],
        scratch=[
            pltpu.VMEM((rows, 2 * TP), BF16),
            pltpu.VMEM(interp_weights.shape, BF16),
            pltpu.SemaphoreType.DMA,
        ],
        flops=2 * 10**9,
    )
    after = lax.ppermute(cyc0, "shot", [((i + 1) % ring, i) for i in range(ring)])
    spec, scale = call(
        scale_kernel,
        [
            jax.ShapeDtypeStruct((HALF * Q_DEV, 2 * TP), F32),
            jax.ShapeDtypeStruct((SLOTS, TP), F32),
        ],
        [cyc0, mask, table],
        flops=10**9,
    )
    return call(
        lambda *refs: correlate_kernel(owners, capacity, *refs),
        jax.ShapeDtypeStruct((shots, Q_DEV, ANG), F32),
        [*late, interp_weights, pick, live, spec, after, scale, table],
        out_specs=HBM,
        scratch=[
            pltpu.VMEM((rows, (shots - 1) * TP), BF16),
            pltpu.VMEM((shots, Q_DEV, ANG), F32),
            pltpu.SemaphoreType.DMA((shots,)),
        ],
    )


def solution(mesh):
    owners = mesh.shape["blk"]
    assert owners & (owners - 1) == 0
    placed = (P("blk", "shot", None), P("blk"), P("blk"), P("blk"), P("blk"), P())
    return jax.shard_map(
        program, mesh=mesh, in_specs=placed, out_specs=P("shot", "blk", None), check_vma=False
    )
```

profile of v0, /device:TPU:0, one launch (start us, length us, event | category | flops | bytes accessed | tf_op | source)
XLA Modules:
  0.0 28.1 jit_solution(12272961175126201792)
XLA Ops:
  0.0 1.6 %shard_map.73 = (bf16[104,128]{1,0:T(8,128)(2,1)S(1)}, bf16[104,128]{1,0:T(8,128)(2,1)S(1)}, bf16[104,128]{1,0:T(8,128)(2,1)S(1)}, bf16[104,128]{1,0:T(8,128)(2,...) custom-call(s32[1]{0:T(128)} %bitcast.refs_0_, ...), custom_call_target="tpu_custom_call" | custom-call | bytes 1048576 | tf_op jit(solution)/shard_map/pallas_call | solution.py:326
  1.7 0.6 %collective-permute-start = (bf16[1152,128]{1,0:T(8,128)(2,1)S(1)}, bf16[1152,128]{1,0:T(8,128)(2,1)S(1)}, u32[]{:S(2)}, u32[]{:S(2)}) collective-permute-start(bf16[1152,128]{1,0:T(8,128)(2,1)S(1)} %get-tuple-element.28), channel_id=1, source_target_pairs={{0,1},{1,0},{2,3},{3,2},{4,5},{5,4},{6,7},{7,6},{8,9},{9,8},{10,11... | collective-permute-start | bytes 884744 | tf_op jit(solution)/shard_map/ppermute | solution.py:342
  2.2 0.1 collective-permute-start.4
  2.3 1.3 %collective-permute-done.4.refs_3_.refs_1_ = bf16[416,128]{1,0:T(8,128)(2,1)S(1)} collective-permute-done((bf16[416,128]{1,0:T(8,128)(2,1)S(1)}, bf16[416,128]{1,0:T(8,128)(2,1)S(1)}, u32[]{:S(2)}, u32[]{:S(2)}) %collective-permute-start.4) | collective-permute-done | bytes 106528 | tf_op jit(solution)/shard_map/ppermute | solution.py:342
  3.6 3.0 %collective-permute-start.5 = (bf16[208,128]{1,0:T(8,128)(2,1)S(1)}, bf16[208,128]{1,0:T(8,128)(2,1)S(1)}, u32[]{:S(2)}, u32[]{:S(2)}) collective-permute-start(bf16[208,128]{1,0:T(8,128)(2,1)S(1)} %get-tuple-element.40), channel_id=1, source_target_pairs={{0,2},{1,3},{2,0},{3,1},{4,6},{5,7},{6,4},{7,5},{8,10},{9,11},{10,... | collective-permute-start | bytes 159752 | tf_op jit(solution)/shard_map/ppermute | solution.py:342
  6.6 2.6 %collective-permute-start.6 = (bf16[208,128]{1,0:T(8,128)(2,1)S(1)}, bf16[208,128]{1,0:T(8,128)(2,1)S(1)}, u32[]{:S(2)}, u32[]{:S(2)}) collective-permute-start(bf16[208,128]{1,0:T(8,128)(2,1)S(1)} %get-tuple-element.41), channel_id=1, source_target_pairs={{0,4},{1,5},{2,6},{3,7},{4,0},{5,1},{6,2},{7,3},{8,12},{9,13},{10,... | collective-permute-start | bytes 159752 | tf_op jit(solution)/shard_map/ppermute | solution.py:342
  9.2 0.0 collective-permute-start.7
  9.2 0.0 collective-permute-done.refs_3_.refs_1_
  9.2 1.0 %collective-permute-start.1 = (bf16[576,128]{1,0:T(8,128)(2,1)S(1)}, bf16[576,128]{1,0:T(8,128)(2,1)S(1)}, u32[]{:S(2)}, u32[]{:S(2)}) collective-permute-start(bf16[576,128]{1,0:T(8,128)(2,1)S(1)} %get-tuple-element.32), channel_id=1, source_target_pairs={{0,2},{1,3},{2,0},{3,1},{4,6},{5,7},{6,4},{7,5},{8,10},{9,11},{10,... | collective-permute-start | bytes 442376 | tf_op jit(solution)/shard_map/ppermute | solution.py:342
  10.2 3.5 %collective-permute-start.2 = (bf16[576,128]{1,0:T(8,128)(2,1)S(1)}, bf16[576,128]{1,0:T(8,128)(2,1)S(1)}, u32[]{:S(2)}, u32[]{:S(2)}) collective-permute-start(bf16[576,128]{1,0:T(8,128)(2,1)S(1)} %get-tuple-element.33), channel_id=1, source_target_pairs={{0,4},{1,5},{2,6},{3,7},{4,0},{5,1},{6,2},{7,3},{8,12},{9,13},{10,... | collective-permute-start | bytes 442376 | tf_op jit(solution)/shard_map/ppermute | solution.py:342
  13.7 0.0 collective-permute-done.5.refs_2_
  13.7 0.0 collective-permute-start.3
  13.7 0.0 collective-permute-done.6.refs_3_
  13.7 2.0 %collective-permute-done.7.refs_4_ = bf16[208,128]{1,0:T(8,128)(2,1)S(1)} collective-permute-done((bf16[208,128]{1,0:T(8,128)(2,1)S(1)}, bf16[208,128]{1,0:T(8,128)(2,1)S(1)}, u32[]{:S(2)}, u32[]{:S(2)}) %collective-permute-start.7) | collective-permute-done | bytes 53280 | tf_op jit(solution)/shard_map/ppermute | solution.py:342
  15.7 0.0 copy-start
  15.7 2.4 %shard_map.76 = (bf16[1024,768]{1,0:T(8,128)(2,1)S(1)}, bf16[768,128]{1,0:T(8,128)(2,1)S(1)}, f32[256,128]{1,0:T(8,128)S(1)}, f32[256,128]{1,0:T(8,128)S(1)}) custom-call(bf16[104,128]{1,0:T(8,128)(2,1)S(1)} %get-tuple-element.35.refs_0_, bf16[416,128]{1,0:T(8,128)(2,1)S(1)} %collective-permute-done.4.refs_3_.refs_1_, ...), custom_call_target="tpu_custom_call" | custom-call | flops 2000000000 | bytes 1048576 | tf_op jit(solution)/shard_map/pallas_call | solution.py:326
  18.1 2.5 %collective-permute-start.8 = (f32[256,128]{1,0:T(8,128)S(1)}, f32[256,128]{1,0:T(8,128)S(1)}, u32[]{:S(2)}, u32[]{:S(2)}) collective-permute-start(f32[256,128]{1,0:T(8,128)S(1)} %get-tuple-element.45.cyc0_ref), channel_id=1, source_target_pairs={{8,0},{16,8},{24,16},{0,24},{9,1},{17,9},{25,17},{1,25},{10,2},{18... | collective-permute-start | bytes 393224 | tf_op jit(solution)/shard_map/ppermute | solution.py:414
  20.6 0.0 copy-done
  20.6 0.0 copy-start.1
  20.6 0.6 %shard_map.77 = (f32[144,256]{1,0:T(8,128)S(1)}, f32[256,128]{1,0:T(8,128)S(1)}) custom-call(f32[256,128]{1,0:T(8,128)S(1)} %get-tuple-element.45.cyc0_ref, f32[256,128]{1,0:T(8,128)S(1)} %get-tuple-element.46.mask_ref, bf16[560,256]{1,0:T(8,128)(2,1)S(1)} %copy-done), custom_call_target="tpu_custom_call" | custom-call | flops 1000000000 | bytes 1048576 | tf_op jit(solution)/shard_map/pallas_call | solution.py:326
  21.3 1.9 %collective-permute-done.8.refs_9_ = f32[256,128]{1,0:T(8,128)S(1)} collective-permute-done((f32[256,128]{1,0:T(8,128)S(1)}, f32[256,128]{1,0:T(8,128)S(1)}, u32[]{:S(2)}, u32[]{:S(2)}) %collective-permute-start.8) | collective-permute-done | bytes 131104 | tf_op jit(solution)/shard_map/ppermute | solution.py:414
  23.1 0.0 collective-permute-done.1.refs_2_
  23.1 1.8 %collective-permute-done.2.refs_3_ = bf16[576,128]{1,0:T(8,128)(2,1)S(1)} collective-permute-done((bf16[576,128]{1,0:T(8,128)(2,1)S(1)}, bf16[576,128]{1,0:T(8,128)(2,1)S(1)}, u32[]{:S(2)}, u32[]{:S(2)}) %collective-permute-start.2) | collective-permute-done | bytes 147488 | tf_op jit(solution)/shard_map/ppermute | solution.py:342
  24.9 0.0 collective-permute-done.3.refs_4_
  24.9 0.0 copy-done.1
  24.9 3.2 %shard_map.78 = f32[4,16,2048]{2,1,0:T(8,128)} custom-call(bf16[288,128]{1,0:T(8,128)(2,1)S(1)} %get-tuple-element.27.refs_0_, bf16[1152,128]{1,0:T(8,128)(2,1)S(1)} %collective-permute-done.refs_3_.refs_1_, bf16[576,128]{1,0:T(8,128)(2,1)S(1)} %collective-permute-done.1.refs_2_, bf16[576,128]{1,0:T(8,128)(2,1)S(1)} %collective-permute-done.2.refs_3_, ...), custom_call_target="tpu_custom_call" | custom-call | bytes 1048576 | tf_op jit(solution)/shard_map/pallas_call | solution.py:326
  (2 shorter events, 0.0 us)
Async XLA Ops:
  1.7 7.5 %collective-permute-start = (bf16[1152,128]{1,0:T(8,128)(2,1)S(1)}, bf16[1152,128]{1,0:T(8,128)(2,1)S(1)}, u32[]{:S(2)}, u32[]{:S(2)}) collective-permute-start(bf16[1152,128]{1,0:T(8,128)(2,1)S(1)} %get-tuple-element.28), channel_id=1, source_target_pairs={{0,1},{1,0},{2,3},{3,2},{4,5},{5,4},{6,7},{7,6},{8,9},{9,8},{10,11... | collective-permute-start | bytes 884744 | tf_op jit(solution)/shard_map/ppermute | solution.py:342
  2.2 1.4 %collective-permute-start.4 = (bf16[416,128]{1,0:T(8,128)(2,1)S(1)}, bf16[416,128]{1,0:T(8,128)(2,1)S(1)}, u32[]{:S(2)}, u32[]{:S(2)}) collective-permute-start(bf16[416,128]{1,0:T(8,128)(2,1)S(1)} %get-tuple-element.36), channel_id=1, source_target_pairs={{0,1},{1,0},{2,3},{3,2},{4,5},{5,4},{6,7},{7,6},{8,9},{9,8},{10,11... | collective-permute-start | bytes 319496 | tf_op jit(solution)/shard_map/ppermute | solution.py:342
  3.6 10.1 %collective-permute-start.5 = (bf16[208,128]{1,0:T(8,128)(2,1)S(1)}, bf16[208,128]{1,0:T(8,128)(2,1)S(1)}, u32[]{:S(2)}, u32[]{:S(2)}) collective-permute-start(bf16[208,128]{1,0:T(8,128)(2,1)S(1)} %get-tuple-element.40), channel_id=1, source_target_pairs={{0,2},{1,3},{2,0},{3,1},{4,6},{5,7},{6,4},{7,5},{8,10},{9,11},{10,... | collective-permute-start | bytes 159752 | tf_op jit(solution)/shard_map/ppermute | solution.py:342
  6.6 7.1 %collective-permute-start.6 = (bf16[208,128]{1,0:T(8,128)(2,1)S(1)}, bf16[208,128]{1,0:T(8,128)(2,1)S(1)}, u32[]{:S(2)}, u32[]{:S(2)}) collective-permute-start(bf16[208,128]{1,0:T(8,128)(2,1)S(1)} %get-tuple-element.41), channel_id=1, source_target_pairs={{0,4},{1,5},{2,6},{3,7},{4,0},{5,1},{6,2},{7,3},{8,12},{9,13},{10,... | collective-permute-start | bytes 159752 | tf_op jit(solution)/shard_map/ppermute | solution.py:342
  9.2 6.5 %collective-permute-start.7 = (bf16[208,128]{1,0:T(8,128)(2,1)S(1)}, bf16[208,128]{1,0:T(8,128)(2,1)S(1)}, u32[]{:S(2)}, u32[]{:S(2)}) collective-permute-start(bf16[208,128]{1,0:T(8,128)(2,1)S(1)} %get-tuple-element.42), channel_id=1, source_target_pairs={{0,6},{1,7},{2,4},{3,5},{4,2},{5,3},{6,0},{7,1},{8,14},{9,15},{10,... | collective-permute-start | bytes 159752 | tf_op jit(solution)/shard_map/ppermute | solution.py:342
  9.2 13.9 %collective-permute-start.1 = (bf16[576,128]{1,0:T(8,128)(2,1)S(1)}, bf16[576,128]{1,0:T(8,128)(2,1)S(1)}, u32[]{:S(2)}, u32[]{:S(2)}) collective-permute-start(bf16[576,128]{1,0:T(8,128)(2,1)S(1)} %get-tuple-element.32), channel_id=1, source_target_pairs={{0,2},{1,3},{2,0},{3,1},{4,6},{5,7},{6,4},{7,5},{8,10},{9,11},{10,... | collective-permute-start | bytes 442376 | tf_op jit(solution)/shard_map/ppermute | solution.py:342
  10.2 14.7 %collective-permute-start.2 = (bf16[576,128]{1,0:T(8,128)(2,1)S(1)}, bf16[576,128]{1,0:T(8,128)(2,1)S(1)}, u32[]{:S(2)}, u32[]{:S(2)}) collective-permute-start(bf16[576,128]{1,0:T(8,128)(2,1)S(1)} %get-tuple-element.33), channel_id=1, source_target_pairs={{0,4},{1,5},{2,6},{3,7},{4,0},{5,1},{6,2},{7,3},{8,12},{9,13},{10,... | collective-permute-start | bytes 442376 | tf_op jit(solution)/shard_map/ppermute | solution.py:342
  13.7 11.3 %collective-permute-start.3 = (bf16[576,128]{1,0:T(8,128)(2,1)S(1)}, bf16[576,128]{1,0:T(8,128)(2,1)S(1)}, u32[]{:S(2)}, u32[]{:S(2)}) collective-permute-start(bf16[576,128]{1,0:T(8,128)(2,1)S(1)} %get-tuple-element.34), channel_id=1, source_target_pairs={{0,6},{1,7},{2,4},{3,5},{4,2},{5,3},{6,0},{7,1},{8,14},{9,15},{10,... | collective-permute-start | bytes 442376 | tf_op jit(solution)/shard_map/ppermute | solution.py:342
  15.7 4.9 %copy-start = (bf16[560,256]{1,0:T(8,128)(2,1)S(1)}, bf16[560,256]{1,0:T(8,128)(2,1)}, u32[]{:S(2)}) copy-start(bf16[560,256]{1,0:T(8,128)(2,1)} %constant.6.clone.table_ref.refs_11_) | copy-start | bytes 860164
  18.1 5.0 %collective-permute-start.8 = (f32[256,128]{1,0:T(8,128)S(1)}, f32[256,128]{1,0:T(8,128)S(1)}, u32[]{:S(2)}, u32[]{:S(2)}) collective-permute-start(f32[256,128]{1,0:T(8,128)S(1)} %get-tuple-element.45.cyc0_ref), channel_id=1, source_target_pairs={{8,0},{16,8},{24,16},{0,24},{9,1},{17,9},{25,17},{1,25},{10,2},{18... | collective-permute-start | bytes 393224 | tf_op jit(solution)/shard_map/ppermute | solution.py:414
  20.6 4.3 %copy-start.1 = (bf16[4,128,128]{2,1,0:T(8,128)(2,1)S(1)}, bf16[4,128,128]{2,1,0:T(8,128)(2,1)}, u32[]{:S(2)}) copy-start(bf16[4,128,128]{2,1,0:T(8,128)(2,1)} %refs_5_.3) | copy-start | bytes 393220
where the time goes:
time: 28.3 us; the launch traced here: 28.1 us
  starting transfers between devices  13.2 us (47%)
  Pallas kernels  7.97 us (28%)
  waiting for transfers between devices  6.95 us (25%)
    ppermute x8, starting transfers between devices, cross(): return lax.ppermute(block, 'blk', [(i, i ^ d) for i in range(owners)])  10.7 us
    pallas_call x6, Pallas kernels, call(): pl.pallas_call(body, out_shape=outs, in_specs=in_specs or [VMEM] * len(op...  7.97 us
    ppermute x8, waiting for transfers between devices, cross(): return lax.ppermute(block, 'blk', [(i, i ^ d) for i in range(owners)])  5.07 us
    ppermute x1, starting transfers between devices, program(): lax.ppermute(cyc0, 'shot', [((i + 1) % ring, i) for i in range(ring)])  2.5 us
    ppermute x1, waiting for transfers between devices, program(): lax.ppermute(cyc0, 'shot', [((i + 1) % ring, i) for i in range(ring)])  1.88 us
  transfers between devices with their start and end apart: 9, of which 4 were waited for; matrix products, arithmetic and copies ran while one was open for 0% of the time, Pallas kernels for 11%

commit v1 on v0

--- a/solution.py
+++ b/solution.py
@@ -18,6 +18,7 @@
 SLOTS = Q_DEV * NSEG
 LANES = 128
 META = 8
+LEAD = 2
 TWIST = 2 * 2 * TP
 ROOT = math.sqrt(0.5)
 COS1, SIN1 = math.cos(math.pi / 8), math.sin(math.pi / 8)
@@ -156,7 +157,7 @@
 def pack_kernel(owners, capacity, me_ref, owner_hbm, place_hbm, kern_hbm, len_hbm, pix_hbm, *rest):
     chips = owners // 2
     first, later = rest[:chips], rest[chips : 2 * chips]
-    swap_first, swap_later, ints, pix, wide, sems = rest[2 * chips :]
+    swap_first, swap_later, lead, ints, pix, wide, sems = rest[2 * chips :]
     tiles = ints.shape[1]
     shots = pix.shape[0] // tiles
     first_rows, later_rows = capacity + META, (shots - 1) * capacity
@@ -180,15 +181,19 @@
             ((place % NSEG) * Q_DEV + place // NSEG).astype(F32),
             (ints[16:17, :] + 1).astype(F32),
             ints[24:25, :].astype(F32),
-            jnp.zeros((META - 3, tiles), F32),
+            jnp.zeros((1, tiles), F32),
         ],
         axis=0,
-    ).astype(BF16)
+    )
+    blank = jnp.zeros_like(meta)
+    metas = [
+        jnp.concatenate(pair, axis=0).astype(BF16) for pair in ((meta, blank), (blank, meta))
+    ]
     placing = [
         (iota((LANES, tiles), 0) + d * LANES == slot).astype(F32).astype(BF16)
         for d in range(owners)
     ]
-    tags = [dot_rows(meta, placing[d]).astype(BF16) for d in range(owners)]
+    tags = [dot_rows(metas[d % 2], placing[d]).astype(BF16) for d in range(owners)]
     copies[4].wait()
     wide[...] = pix[...].astype(F32)
     pixels = jnp.concatenate(
@@ -205,68 +210,81 @@
         near[at + capacity : at + first_rows, :] = tags[d]
         for s in range(1, shots):
             start = to + (s - 1) * capacity
-            far[start : start + capacity, :] = sent[:, s * TP : (s + 1) * TP]
-
-
-def merge_kernel(chips, *refs):
+            out = far
+            if d == owners // 2 and s >= shots - LEAD:
+                out, start = lead, (s + LEAD - shots) * capacity
+            out[start : start + capacity, :] = sent[:, s * TP : (s + 1) * TP]
+
+
+def merge_kernel(chips, shared, *refs):
     own, other, outs = refs[: chips - 1], refs[chips - 1], refs[chips:]
-    rows = own[0].shape[0]
+    size = other.shape[0] // chips
+    body = size - shared
     for j in range(1, chips):
-        outs[j - 1][:rows, :] = own[j - 1][...]
-        outs[j - 1][rows:, :] = other[j * rows : (j + 1) * rows, :]
-
-
-def sources(own, other, far, rows):
-    blocks = [own, other.at[pl.ds(0, rows), :]]
-    for ref in far:
-        blocks += [ref.at[pl.ds(0, rows), :], ref.at[pl.ds(rows, rows), :]]
-    return blocks
-
-
-def weigh(sums, count, weights_ref):
+        block, start, out = own[j - 1], j * size, outs[j - 1]
+        first = block.shape[0] - shared
+        out[:first, :] = block[:first, :]
+        out[first : first + body, :] = other[start : start + body, :]
+        if shared:
+            out[first + body :, :] = block[first:, :] + other[start + body : start + size, :]
+
+
+def interpolate(pixels, kern, weights_ref):
     kernels = weights_ref.shape[0]
-    weights = weights_ref[...].reshape(kernels * TP, TP)
-    cycles = []
-    for s in range(count):
-        columns = slice(s * TP, (s + 1) * TP)
-        high, low = split(
-            jnp.concatenate(
-                [sums[k * SLOTS : (k + 1) * SLOTS, columns] for k in range(kernels)], axis=1
-            )
-        )
-        cycles.append(dot(high, weights) + dot(low, weights))
-    return cycles
+    weights = jnp.concatenate([weights_ref[k] for k in range(kernels)], axis=1)
+    every = dot(pixels, weights)
+    value = every[:, :TP]
+    for k in range(1, kernels):
+        value = jnp.where(kern == k + 1.0, every[:, k * TP : (k + 1) * TP], value)
+    return value
+
+
+def scatter(pick, values):
+    halves = [half for value in values for half in split(value)]
+    sums = dot(pick, jnp.concatenate(halves, axis=1))
+    return [
+        sums[:, 2 * s * TP : (2 * s + 1) * TP] + sums[:, (2 * s + 1) * TP : (2 * s + 2) * TP]
+        for s in range(len(values))
+    ]
 
 
 def gather_kernel(owners, capacity, *refs):
-    weights_hbm, pick_ref, live_ref, cyc0_ref, mask_ref, table, weights_ref, sem = refs[-8:]
+    weights_hbm, pick_ref, live_ref, kern_ref, cyc0_ref, mask_ref, weights_ref, sem = refs[-8:]
     copy = pltpu.make_async_copy(weights_hbm, weights_ref, sem)
     copy.start()
-    got = sources(refs[0], refs[1], refs[2:-8], capacity + META)
-    kernels = weights_ref.shape[0]
-    metas = [g[capacity : capacity + META, :].astype(F32) for g in got]
-    group = math.gcd(owners, 8)
+    got, metas = [], []
+    for j in range(owners // 2):
+        for core in range(2):
+            ref = refs[core] if j == 0 else refs[j + 1]
+            start = core * capacity if j else 0
+            tags = ref[ref.shape[0] - META :, :] if j else ref[capacity : capacity + META, :]
+            got.append(ref.at[pl.ds(start, capacity), :])
+            metas.append(tags.astype(F32)[4 * core : 4 * core + 4])
+    group = math.gcd(owners, 4)
     for base in range(0, owners, group):
-        lens = jnp.concatenate([m[2:3] for m in metas[base : base + group]], axis=0)
-        lens = jnp.transpose(lens)
+        tags = jnp.concatenate([m[1:3] for m in metas[base : base + group]], axis=0)
+        if group < 4:
+            tags = jnp.concatenate([tags, jnp.zeros((8 - 2 * group, LANES), F32)], axis=0)
+        tags = jnp.transpose(tags)
         for i in range(group):
-            d = base + i
-            rows = slice(d * capacity, (d + 1) * capacity)
-            live = iota((capacity, TP), 1).astype(F32) < lens[:capacity, i : i + 1]
-            live = jnp.where(live, 1.0, 0.0).astype(BF16)
-            live_ref[rows, :] = live
-            table[rows, :TP] = got[d][:capacity, :] * live
-            table[rows, TP:] = live
-    index = [
-        jnp.where(m[1:2] > 0.5, m[0:1] + (m[1:2] - 1.0) * SLOTS, -1.0)[:, :capacity] for m in metas
-    ]
-    index = jnp.concatenate(index, axis=1).astype(jnp.int32)
-    hit = iota((kernels * SLOTS, owners * capacity), 0) == index
-    pick = hit.astype(F32).astype(BF16)
-    pick_ref[...] = pick
-    sums = dot(pick, table[...])
+            rows = slice((base + i) * capacity, (base + i + 1) * capacity)
+            kern_ref[rows, :] = jnp.broadcast_to(
+                tags[:capacity, 2 * i : 2 * i + 1], (capacity, TP)
+            )
+            live = iota((capacity, TP), 1).astype(F32) < tags[:capacity, 2 * i + 1 : 2 * i + 2]
+            live_ref[rows, :] = jnp.where(live, 1.0, 0.0).astype(BF16)
+    place = [jnp.where(m[1:2] > 0.5, m[0:1], -1.0)[:, :capacity] for m in metas]
+    place = jnp.broadcast_to(jnp.concatenate(place, axis=1), (SLOTS, owners * capacity))
+    slot = iota((SLOTS, owners * capacity), 0).astype(F32).astype(BF16)
+    one = jnp.ones(slot.shape, BF16)
+    pick_ref[...] = jnp.where(slot == place.astype(BF16), one, jnp.zeros_like(one))
+    live, kern = live_ref[...], kern_ref[...]
+    pixels = jnp.concatenate([g[...] for g in got], axis=0) * live
     copy.wait()
-    cyc0_ref[...], mask_ref[...] = weigh(sums, 2, weights_ref)
+    cyc0_ref[...], mask_ref[...] = scatter(
+        pick_ref[...],
+        [interpolate(pixels, kern, weights_ref), interpolate(live, kern, weights_ref)],
+    )
 
 
 def scale_kernel(cyc0_ref, mask_ref, table_ref, spec_ref, scale_ref):
@@ -282,20 +300,55 @@
         scale_ref[m * Q_DEV : (m + 1) * Q_DEV, :] = (2.0 / ANG) / whole
 
 
-def correlate_kernel(owners, capacity, *refs):
-    (weights_ref, pick_ref, live_ref, spec_ref, next_ref, scale_ref, table_ref, out_hbm, table,
-     out, sems) = refs[-11:]
+def late_blocks(far, capacity, shots, lead=None):
+    blocks = []
+    for ref in far:
+        for core in range(2):
+            start = core * (ref.shape[0] - shots * capacity)
+            held = shots if lead is None or blocks else shots - LEAD
+            block = [ref.at[pl.ds(start + s * capacity, capacity), :] for s in range(held)]
+            block += [
+                lead.at[pl.ds(s * capacity, capacity), :] for s in range(shots - held)
+            ]
+            blocks.append(block)
+    return blocks
+
+
+def late_cycles(blocks, live_ref, kern_ref, pick_ref, weights_ref, first):
+    count = sum(ref.shape[0] for ref in blocks[0])
+    capacity = count // len(blocks[0])
+    rows = slice(first, first + capacity * len(blocks))
+    live, kern = live_ref[rows, :], kern_ref[rows, :]
+    values = [
+        interpolate(
+            jnp.concatenate([block[s][...] for block in blocks], axis=0) * live, kern, weights_ref
+        )
+        for s in range(len(blocks[0]))
+    ]
+    return scatter(pick_ref[:, rows], values)
+
+
+def partial_kernel(capacity, shots, own, other, *refs):
+    (weights_ref, pick_ref, live_ref, kern_ref, next_ref, table_ref, part_ref, spec_ref) = refs[-8:]
+    blocks = [
+        [ref.at[pl.ds(s * capacity, capacity), :] for s in range(shots)] for ref in (own, other)
+    ]
+    blocks += late_blocks(refs[:-8], capacity, shots)
+    cycles = late_cycles(blocks, live_ref, kern_ref, pick_ref, weights_ref, 0)
+    for s, cycle in enumerate(cycles):
+        part_ref[:, s * TP : (s + 1) * TP] = cycle
+    spec_ref[...] = spectrum([next_ref[...]], table_ref)
+
+
+def correlate_kernel(capacity, lead, *refs):
+    (weights_ref, pick_ref, live_ref, kern_ref, part_ref, spec_ref, next_ref, scale_ref, table_ref,
+     out_hbm, out, sems) = refs[-12:]
     shots = out.shape[0]
-    got = sources(refs[0], refs[1], refs[2:-11], (shots - 1) * capacity)
-    for d in range(owners):
-        rows = slice(d * capacity, (d + 1) * capacity)
-        live = live_ref[rows, :]
-        for s in range(shots - 1):
-            table[rows, s * TP : (s + 1) * TP] = (
-                got[d][s * capacity : (s + 1) * capacity, :] * live
-            )
-    cycles = weigh(dot(pick_ref[...], table[...]), shots - 1, weights_ref)
-    spec = jnp.concatenate([spec_ref[...], spectrum(cycles + [next_ref[...]], table_ref)], axis=0)
+    blocks = late_blocks(refs[:-12], capacity, shots - 1, lead)
+    first = live_ref.shape[0] - capacity * len(blocks)
+    cycles = late_cycles(blocks, live_ref, kern_ref, pick_ref, weights_ref, first)
+    cycles = [c + part_ref[:, s * TP : (s + 1) * TP] for s, c in enumerate(cycles)]
+    spec = jnp.concatenate([spec_ref[...], spectrum(cycles, table_ref), next_ref[...]], axis=0)
     rows = HALF * Q_DEV
     diff = spec[: shots * rows] - spec[rows:]
     spec = spec[: shots * rows]
@@ -342,17 +395,17 @@
     return lax.ppermute(block, "blk", [(i, i ^ d) for i in range(owners)])
 
 
-def exchange(own, swap, owners):
+def exchange(own, swap, owners, shared):
     chips = owners // 2
     other = cross(swap, 1, owners)
-    rows = own[0].shape[0]
+    size = swap.shape[0] // chips - shared
     merged = call(
-        lambda *refs: merge_kernel(chips, *refs),
-        [jax.ShapeDtypeStruct((2 * rows, TP), BF16)] * (chips - 1),
+        lambda *refs: merge_kernel(chips, shared, *refs),
+        [jax.ShapeDtypeStruct((block.shape[0] + size, TP), BF16) for block in own[1:]],
         [*own[1:], other],
     )
     far = {d: cross(merged[d // 2 - 1], d, owners) for d in far_order(owners)}
-    return [own[0], other] + [far[d] for d in range(2, owners, 2)]
+    return own[0], other, [far[d] for d in range(2, owners, 2)]
 
 
 def program(intensities, tile_owner, tile_place, tile_kernel, mask_len, interp_weights):
@@ -360,7 +413,6 @@
     chips = owners // 2
     ring = lax.axis_size("shot")
     tiles, shots, _ = intensities.shape
-    kernels = interp_weights.shape[0]
     capacity = -(-(3 * tiles // owners) // 16) * 16
     rows = owners * capacity
     table = jnp.asarray(dft_table())
@@ -368,9 +420,13 @@
     sent = call(
         lambda *refs: pack_kernel(owners, capacity, *refs),
         [jax.ShapeDtypeStruct((capacity + META, TP), BF16)] * chips
-        + [jax.ShapeDtypeStruct(((shots - 1) * capacity, TP), BF16)] * chips
+        + [
+            jax.ShapeDtypeStruct(((shots - 1 - LEAD * (4 * j == owners)) * capacity, TP), BF16)
+            for j in range(chips)
+        ]
         + [jax.ShapeDtypeStruct((chips * (capacity + META), TP), BF16)]
-        + [jax.ShapeDtypeStruct((chips * (shots - 1) * capacity, TP), BF16)],
+        + [jax.ShapeDtypeStruct((chips * (shots - 1) * capacity, TP), BF16)]
+        + [jax.ShapeDtypeStruct((LEAD * capacity, TP), BF16)],
         [
             me,
             *(
@@ -392,23 +448,24 @@
             pltpu.SemaphoreType.DMA((5,)),
         ],
     )
-    early = exchange(sent[:chips], sent[2 * chips], owners)
-    late = exchange(sent[chips : 2 * chips], sent[2 * chips + 1], owners)
-    pick, live, cyc0, mask = call(
+    lead = cross(sent[-1], owners // 2, owners)
+    own, other, far = exchange(sent[:chips], sent[2 * chips], owners, META)
+    last = chips // 2 - 1
+    early = [own, other, *far[:last], *far[last + 1 :], far[last]]
+    own, other, far = exchange(sent[chips : 2 * chips], sent[2 * chips + 1], owners, 0)
+    near, far = far[:last] + far[last + 1 :], far[last : last + 1]
+    pick, live, kern, cyc0, mask = call(
         lambda *refs: gather_kernel(owners, capacity, *refs),
         [
-            jax.ShapeDtypeStruct((kernels * SLOTS, rows), BF16),
+            jax.ShapeDtypeStruct((SLOTS, rows), BF16),
             jax.ShapeDtypeStruct((rows, TP), BF16),
+            jax.ShapeDtypeStruct((rows, TP), F32),
             jax.ShapeDtypeStruct((SLOTS, TP), F32),
             jax.ShapeDtypeStruct((SLOTS, TP), F32),
         ],
         [*early, pltpu.with_memory_space_constraint(interp_weights, pltpu.HBM)],
         in_specs=[VMEM] * len(early) + [HBM],
-        scratch=[
-            pltpu.VMEM((rows, 2 * TP), BF16),
-            pltpu.VMEM(interp_weights.shape, BF16),
-            pltpu.SemaphoreType.DMA,
-        ],
+        scratch=[pltpu.VMEM(interp_weights.shape, BF16), pltpu.SemaphoreType.DMA],
         flops=2 * 10**9,
     )
     after = lax.ppermute(cyc0, "shot", [((i + 1) % ring, i) for i in range(ring)])
@@ -421,13 +478,21 @@
         [cyc0, mask, table],
         flops=10**9,
     )
+    part, after = call(
+        lambda *refs: partial_kernel(capacity, shots - 1, *refs),
+        [
+            jax.ShapeDtypeStruct((SLOTS, (shots - 1) * TP), F32),
+            jax.ShapeDtypeStruct((HALF * Q_DEV, 2 * TP), F32),
+        ],
+        [own, other, *near, interp_weights, pick, live, kern, after, table],
+        flops=10**9,
+    )
     return call(
-        lambda *refs: correlate_kernel(owners, capacity, *refs),
+        lambda *refs: correlate_kernel(capacity, *refs),
         jax.ShapeDtypeStruct((shots, Q_DEV, ANG), F32),
-        [*late, interp_weights, pick, live, spec, after, scale, table],
+        [lead, *far, interp_weights, pick, live, kern, part, spec, after, scale, table],
         out_specs=HBM,
         scratch=[
-            pltpu.VMEM((rows, (shots - 1) * TP), BF16),
             pltpu.VMEM((shots, Q_DEV, ANG), F32),
             pltpu.SemaphoreType.DMA((shots,)),
         ],

time: 28.3 us -> 29.9 us (1.057)
  starting transfers between devices: 13.2 us -> 16 us
  Pallas kernels: 7.97 us -> 7.03 us
  waiting for transfers between devices: 6.95 us -> 6.38 us
    ppermute x8 -> x9, starting transfers between devices: 10.7 us -> 13.5 us  [cross(): return lax.ppermute(block, 'blk', [(i, i ^ d) for i in range(owners)])]
    ppermute x1, waiting for transfers between devices: 1.88 us -> 0.01 us  [program(): lax.ppermute(cyc0, 'shot', [((i + 1) % ring, i) for i in range(ring)])]
    ppermute x8 -> x9, waiting for transfers between devices: 5.07 us -> 6.38 us  [cross(): return lax.ppermute(block, 'blk', [(i, i ^ d) for i in range(owners)])]
    pallas_call x6 -> x7, Pallas kernels: 7.97 us -> 7.03 us  [call(): pl.pallas_call(body, out_shape=outs, in_specs=in_specs or [VMEM] * len(op...]
  transfers between devices with their start and end apart: 9 -> 10, of which waited for: 4 -> 4; matrix products, arithmetic and copies ran while one was open for 0% -> 0% of each run, Pallas kernels for 11% -> 11%
where the time goes in v1:
time: 29.9 us; the launch traced here: 29.7 us
  starting transfers between devices  16 us (54%)
  Pallas kernels  7.03 us (24%)
  waiting for transfers between devices  6.38 us (21%)
    ppermute x9, starting transfers between devices, cross(): return lax.ppermute(block, 'blk', [(i, i ^ d) for i in range(owners)])  13.5 us
    pallas_call x7, Pallas kernels, call(): pl.pallas_call(body, out_shape=outs, in_specs=in_specs or [VMEM] * len(op...  7.03 us
    ppermute x9, waiting for transfers between devices, cross(): return lax.ppermute(block, 'blk', [(i, i ^ d) for i in range(owners)])  6.38 us
    ppermute x1, starting transfers between devices, program(): lax.ppermute(cyc0, 'shot', [((i + 1) % ring, i) for i in range(ring)])  2.5 us
  transfers between devices with their start and end apart: 10, of which 4 were waited for; matrix products, arithmetic and copies ran while one was open for 0% of the time, Pallas kernels for 11%

profile of v1, /device:TPU:0, one launch (start us, length us, event | category | flops | bytes accessed | tf_op | source)
XLA Modules:
  0.0 29.7 jit_solution(12016389596905728960)
XLA Ops:
  0.0 1.6 %shard_map.73 = (bf16[104,128]{1,0:T(8,128)(2,1)S(1)}, bf16[104,128]{1,0:T(8,128)(2,1)S(1)}, bf16[104,128]{1,0:T(8,128)(2,1)S(1)}, bf16[104,128]{1,0:T(8,128)(2,...) custom-call(s32[1]{0:T(128)} %bitcast.refs_0_, ...), custom_call_target="tpu_custom_call" | custom-call | bytes 1048576 | tf_op jit(solution)/shard_map/pallas_call | solution.py:379
  1.7 0.6 %collective-permute-start.1 = (bf16[1152,128]{1,0:T(8,128)(2,1)S(1)}, bf16[1152,128]{1,0:T(8,128)(2,1)S(1)}, u32[]{:S(2)}, u32[]{:S(2)}) collective-permute-start(bf16[1152,128]{1,0:T(8,128)(2,1)S(1)} %get-tuple-element.35), channel_id=1, source_target_pairs={{0,1},{1,0},{2,3},{3,2},{4,5},{5,4},{6,7},{7,6},{8,9},{9,8},{10,11... | collective-permute-start | bytes 884744 | tf_op jit(solution)/shard_map/ppermute | solution.py:395
  2.2 0.1 collective-permute-start.3
  2.3 1.3 %collective-permute-done.3.refs_3_.refs_1_ = bf16[416,128]{1,0:T(8,128)(2,1)S(1)} collective-permute-done((bf16[416,128]{1,0:T(8,128)(2,1)S(1)}, bf16[416,128]{1,0:T(8,128)(2,1)S(1)}, u32[]{:S(2)}, u32[]{:S(2)}) %collective-permute-start.3) | collective-permute-done | bytes 106528 | tf_op jit(solution)/shard_map/ppermute | solution.py:395
  3.6 3.0 %collective-permute-start.4 = (bf16[200,128]{1,0:T(8,128)(2,1)S(1)}, bf16[200,128]{1,0:T(8,128)(2,1)S(1)}, u32[]{:S(2)}, u32[]{:S(2)}) collective-permute-start(bf16[200,128]{1,0:T(8,128)(2,1)S(1)} %get-tuple-element.42), channel_id=1, source_target_pairs={{0,2},{1,3},{2,0},{3,1},{4,6},{5,7},{6,4},{7,5},{8,10},{9,11},{10,... | collective-permute-start | bytes 153608 | tf_op jit(solution)/shard_map/ppermute | solution.py:395
  6.6 2.5 %collective-permute-start.5 = (bf16[200,128]{1,0:T(8,128)(2,1)S(1)}, bf16[200,128]{1,0:T(8,128)(2,1)S(1)}, u32[]{:S(2)}, u32[]{:S(2)}) collective-permute-start(bf16[200,128]{1,0:T(8,128)(2,1)S(1)} %get-tuple-element.43), channel_id=1, source_target_pairs={{0,6},{1,7},{2,4},{3,5},{4,2},{5,3},{6,0},{7,1},{8,14},{9,15},{10,... | collective-permute-start | bytes 153608 | tf_op jit(solution)/shard_map/ppermute | solution.py:395
  9.1 0.1 collective-permute-start.6
  9.2 0.0 collective-permute-done.1.refs_3_.refs_1_
  9.2 1.9 %collective-permute-start.7 = (bf16[576,128]{1,0:T(8,128)(2,1)S(1)}, bf16[576,128]{1,0:T(8,128)(2,1)S(1)}, u32[]{:S(2)}, u32[]{:S(2)}) collective-permute-start(bf16[576,128]{1,0:T(8,128)(2,1)S(1)} %get-tuple-element.49), channel_id=1, source_target_pairs={{0,2},{1,3},{2,0},{3,1},{4,6},{5,7},{6,4},{7,5},{8,10},{9,11},{10,... | collective-permute-start | bytes 442376 | tf_op jit(solution)/shard_map/ppermute | solution.py:395
  11.1 2.5 %collective-permute-start.8 = (bf16[576,128]{1,0:T(8,128)(2,1)S(1)}, bf16[576,128]{1,0:T(8,128)(2,1)S(1)}, u32[]{:S(2)}, u32[]{:S(2)}) collective-permute-start(bf16[576,128]{1,0:T(8,128)(2,1)S(1)} %get-tuple-element.50), channel_id=1, source_target_pairs={{0,6},{1,7},{2,4},{3,5},{4,2},{5,3},{6,0},{7,1},{8,14},{9,15},{10,... | collective-permute-start | bytes 442376 | tf_op jit(solution)/shard_map/ppermute | solution.py:395
  13.6 0.0 collective-permute-done.4.refs_2_
  13.6 0.0 collective-permute-done.5.refs_3_
  13.6 1.6 %collective-permute-done.6.refs_4_ = bf16[200,128]{1,0:T(8,128)(2,1)S(1)} collective-permute-done((bf16[200,128]{1,0:T(8,128)(2,1)S(1)}, bf16[200,128]{1,0:T(8,128)(2,1)S(1)}, u32[]{:S(2)}, u32[]{:S(2)}) %collective-permute-start.6) | collective-permute-done | bytes 51232 | tf_op jit(solution)/shard_map/ppermute | solution.py:395
  15.2 0.0 copy-start
  15.2 1.7 %shard_map.76 = (bf16[256,768]{1,0:T(8,128)(2,1)S(1)}, bf16[768,128]{1,0:T(8,128)(2,1)S(1)}, f32[768,128]{1,0:T(8,128)S(1)}, f32[256,128]{1,0:T(8,128)S(1)}, f32[256,128]{1,0:T(8,128)S(1)}) custom-call(bf16[104,128]{1,0:T(8,128)(2,1)S(1)} %get-tuple-element.37.refs_0_, bf16[416,128]{1,0:T(8,128)(2,1)S(1)} %collective-permute-done.3.refs_3_.refs_1_, ...), custom_call_target="tpu_custom_call" | custom-call | flops 2000000000 | bytes 1048576 | tf_op jit(solution)/shard_map/pallas_call | solution.py:379
  16.9 2.5 %collective-permute-start.9 = (f32[256,128]{1,0:T(8,128)S(1)}, f32[256,128]{1,0:T(8,128)S(1)}, u32[]{:S(2)}, u32[]{:S(2)}) collective-permute-start(f32[256,128]{1,0:T(8,128)S(1)} %get-tuple-element.51.cyc0_ref), channel_id=1, source_target_pairs={{8,0},{16,8},{24,16},{0,24},{9,1},{17,9},{25,17},{1,25},{10,2},{18... | collective-permute-start | bytes 393224 | tf_op jit(solution)/shard_map/ppermute | solution.py:471
  19.4 0.5 %collective-permute-start = (bf16[192,128]{1,0:T(8,128)(2,1)S(1)}, bf16[192,128]{1,0:T(8,128)(2,1)S(1)}, u32[]{:S(2)}, u32[]{:S(2)}) collective-permute-start(bf16[192,128]{1,0:T(8,128)(2,1)S(1)} %get-tuple-element.31), channel_id=1, source_target_pairs={{0,4},{1,5},{2,6},{3,7},{4,0},{5,1},{6,2},{7,3},{8,12},{9,13},{10,... | collective-permute-start | bytes 147464 | tf_op jit(solution)/shard_map/ppermute | solution.py:395
  19.9 2.4 %collective-permute-start.2 = (bf16[384,128]{1,0:T(8,128)(2,1)S(1)}, bf16[384,128]{1,0:T(8,128)(2,1)S(1)}, u32[]{:S(2)}, u32[]{:S(2)}) collective-permute-start(bf16[384,128]{1,0:T(8,128)(2,1)S(1)} %get-tuple-element.36), channel_id=1, source_target_pairs={{0,4},{1,5},{2,6},{3,7},{4,0},{5,1},{6,2},{7,3},{8,12},{9,13},{10,... | collective-permute-start | bytes 294920 | tf_op jit(solution)/shard_map/ppermute | solution.py:395
  22.3 0.0 copy-done
  22.3 0.0 copy-start.1
  22.3 0.6 %shard_map.78 = (f32[144,256]{1,0:T(8,128)S(1)}, f32[256,128]{1,0:T(8,128)S(1)}) custom-call(f32[256,128]{1,0:T(8,128)S(1)} %get-tuple-element.51.cyc0_ref, f32[256,128]{1,0:T(8,128)S(1)} %get-tuple-element.53.mask_ref, bf16[560,256]{1,0:T(8,128)(2,1)S(1)} %copy-done), custom_call_target="tpu_custom_call" | custom-call | flops 1000000000 | bytes 1048576 | tf_op jit(solution)/shard_map/pallas_call | solution.py:379
  23.0 0.0 collective-permute-done.9.refs_8_
  23.0 0.0 collective-permute-done.7.refs_2_
  23.0 0.0 collective-permute-done.8.refs_3_
  23.0 0.2 copy-done.1
  23.2 1.0 %shard_map.77 = (f32[256,384]{1,0:T(8,128)S(1)}, f32[144,256]{1,0:T(8,128)S(1)}) custom-call(bf16[288,128]{1,0:T(8,128)(2,1)S(1)} %get-tuple-element.48.refs_0_, bf16[1152,128]{1,0:T(8,128)(2,1)S(1)} %collective-permute-done.1.refs_3_.refs_1_, bf16[576,128]{1,0:T(8,128)(2,1)S(1)} %collective-permute-done.7.refs_2_, ...), custom_call_target="tpu_custom_call" | custom-call | flops 1000000000 | bytes 1048576 | tf_op jit(solution)/shard_map/pallas_call | solution.py:379
  24.2 1.4 %collective-permute-done.refs_0_ = bf16[192,128]{1,0:T(8,128)(2,1)S(1)} collective-permute-done((bf16[192,128]{1,0:T(8,128)(2,1)S(1)}, bf16[192,128]{1,0:T(8,128)(2,1)S(1)}, u32[]{:S(2)}, u32[]{:S(2)}) %collective-permute-start) | collective-permute-done | bytes 49184 | tf_op jit(solution)/shard_map/ppermute | solution.py:395
  25.6 2.1 %collective-permute-done.2.refs_1_ = bf16[384,128]{1,0:T(8,128)(2,1)S(1)} collective-permute-done((bf16[384,128]{1,0:T(8,128)(2,1)S(1)}, bf16[384,128]{1,0:T(8,128)(2,1)S(1)}, u32[]{:S(2)}, u32[]{:S(2)}) %collective-permute-start.2) | collective-permute-done | bytes 98336 | tf_op jit(solution)/shard_map/ppermute | solution.py:395
  27.7 2.0 %shard_map.79 = f32[4,16,2048]{2,1,0:T(8,128)} custom-call(bf16[192,128]{1,0:T(8,128)(2,1)S(1)} %collective-permute-done.refs_0_, bf16[384,128]{1,0:T(8,128)(2,1)S(1)} %collective-permute-done.2.refs_1_, bf16[4,128,128]{2,1,0:T(8,128)(2,1)S(1)} %copy-done.1, bf16[256,768]{1,0:T(8,128)(2,1)S(1)} %get-tuple-element.45.refs_5_.refs_3_, ...), custom_call_target="tpu_custom_call" | custom-call | bytes 1048576 | tf_op jit(solution)/shard_map/pallas_call | solution.py:379
  (2 shorter events, 0.0 us)
Async XLA Ops:
  1.7 7.5 %collective-permute-start.1 = (bf16[1152,128]{1,0:T(8,128)(2,1)S(1)}, bf16[1152,128]{1,0:T(8,128)(2,1)S(1)}, u32[]{:S(2)}, u32[]{:S(2)}) collective-permute-start(bf16[1152,128]{1,0:T(8,128)(2,1)S(1)} %get-tuple-element.35), channel_id=1, source_target_pairs={{0,1},{1,0},{2,3},{3,2},{4,5},{5,4},{6,7},{7,6},{8,9},{9,8},{10,11... | collective-permute-start | bytes 884744 | tf_op jit(solution)/shard_map/ppermute | solution.py:395
  2.2 1.4 %collective-permute-start.3 = (bf16[416,128]{1,0:T(8,128)(2,1)S(1)}, bf16[416,128]{1,0:T(8,128)(2,1)S(1)}, u32[]{:S(2)}, u32[]{:S(2)}) collective-permute-start(bf16[416,128]{1,0:T(8,128)(2,1)S(1)} %get-tuple-element.38), channel_id=1, source_target_pairs={{0,1},{1,0},{2,3},{3,2},{4,5},{5,4},{6,7},{7,6},{8,9},{9,8},{10,11... | collective-permute-start | bytes 319496 | tf_op jit(solution)/shard_map/ppermute | solution.py:395
  3.6 10.0 %collective-permute-start.4 = (bf16[200,128]{1,0:T(8,128)(2,1)S(1)}, bf16[200,128]{1,0:T(8,128)(2,1)S(1)}, u32[]{:S(2)}, u32[]{:S(2)}) collective-permute-start(bf16[200,128]{1,0:T(8,128)(2,1)S(1)} %get-tuple-element.42), channel_id=1, source_target_pairs={{0,2},{1,3},{2,0},{3,1},{4,6},{5,7},{6,4},{7,5},{8,10},{9,11},{10,... | collective-permute-start | bytes 153608 | tf_op jit(solution)/shard_map/ppermute | solution.py:395
  6.6 7.0 %collective-permute-start.5 = (bf16[200,128]{1,0:T(8,128)(2,1)S(1)}, bf16[200,128]{1,0:T(8,128)(2,1)S(1)}, u32[]{:S(2)}, u32[]{:S(2)}) collective-permute-start(bf16[200,128]{1,0:T(8,128)(2,1)S(1)} %get-tuple-element.43), channel_id=1, source_target_pairs={{0,6},{1,7},{2,4},{3,5},{4,2},{5,3},{6,0},{7,1},{8,14},{9,15},{10,... | collective-permute-start | bytes 153608 | tf_op jit(solution)/shard_map/ppermute | solution.py:395
  9.1 6.1 %collective-permute-start.6 = (bf16[200,128]{1,0:T(8,128)(2,1)S(1)}, bf16[200,128]{1,0:T(8,128)(2,1)S(1)}, u32[]{:S(2)}, u32[]{:S(2)}) collective-permute-start(bf16[200,128]{1,0:T(8,128)(2,1)S(1)} %get-tuple-element.44), channel_id=1, source_target_pairs={{0,4},{1,5},{2,6},{3,7},{4,0},{5,1},{6,2},{7,3},{8,12},{9,13},{10,... | collective-permute-start | bytes 153608 | tf_op jit(solution)/shard_map/ppermute | solution.py:395
  9.2 13.8 %collective-permute-start.7 = (bf16[576,128]{1,0:T(8,128)(2,1)S(1)}, bf16[576,128]{1,0:T(8,128)(2,1)S(1)}, u32[]{:S(2)}, u32[]{:S(2)}) collective-permute-start(bf16[576,128]{1,0:T(8,128)(2,1)S(1)} %get-tuple-element.49), channel_id=1, source_target_pairs={{0,2},{1,3},{2,0},{3,1},{4,6},{5,7},{6,4},{7,5},{8,10},{9,11},{10,... | collective-permute-start | bytes 442376 | tf_op jit(solution)/shard_map/ppermute | solution.py:395
  11.1 11.9 %collective-permute-start.8 = (bf16[576,128]{1,0:T(8,128)(2,1)S(1)}, bf16[576,128]{1,0:T(8,128)(2,1)S(1)}, u32[]{:S(2)}, u32[]{:S(2)}) collective-permute-start(bf16[576,128]{1,0:T(8,128)(2,1)S(1)} %get-tuple-element.50), channel_id=1, source_target_pairs={{0,6},{1,7},{2,4},{3,5},{4,2},{5,3},{6,0},{7,1},{8,14},{9,15},{10,... | collective-permute-start | bytes 442376 | tf_op jit(solution)/shard_map/ppermute | solution.py:395
  15.2 7.2 %copy-start = (bf16[560,256]{1,0:T(8,128)(2,1)S(1)}, bf16[560,256]{1,0:T(8,128)(2,1)}, u32[]{:S(2)}) copy-start(bf16[560,256]{1,0:T(8,128)(2,1)} %constant.6.clone.refs_9_.table_ref.refs_10_) | copy-start | bytes 860164
  16.9 6.1 %collective-permute-start.9 = (f32[256,128]{1,0:T(8,128)S(1)}, f32[256,128]{1,0:T(8,128)S(1)}, u32[]{:S(2)}, u32[]{:S(2)}) collective-permute-start(f32[256,128]{1,0:T(8,128)S(1)} %get-tuple-element.51.cyc0_ref), channel_id=1, source_target_pairs={{8,0},{16,8},{24,16},{0,24},{9,1},{17,9},{25,17},{1,25},{10,2},{18... | collective-permute-start | bytes 393224 | tf_op jit(solution)/shard_map/ppermute | solution.py:471
  19.4 6.2 %collective-permute-start = (bf16[192,128]{1,0:T(8,128)(2,1)S(1)}, bf16[192,128]{1,0:T(8,128)(2,1)S(1)}, u32[]{:S(2)}, u32[]{:S(2)}) collective-permute-start(bf16[192,128]{1,0:T(8,128)(2,1)S(1)} %get-tuple-element.31), channel_id=1, source_target_pairs={{0,4},{1,5},{2,6},{3,7},{4,0},{5,1},{6,2},{7,3},{8,12},{9,13},{10,... | collective-permute-start | bytes 147464 | tf_op jit(solution)/shard_map/ppermute | solution.py:395
  19.9 7.7 %collective-permute-start.2 = (bf16[384,128]{1,0:T(8,128)(2,1)S(1)}, bf16[384,128]{1,0:T(8,128)(2,1)S(1)}, u32[]{:S(2)}, u32[]{:S(2)}) collective-permute-start(bf16[384,128]{1,0:T(8,128)(2,1)S(1)} %get-tuple-element.36), channel_id=1, source_target_pairs={{0,4},{1,5},{2,6},{3,7},{4,0},{5,1},{6,2},{7,3},{8,12},{9,13},{10,... | collective-permute-start | bytes 294920 | tf_op jit(solution)/shard_map/ppermute | solution.py:395
  22.3 0.9 %copy-start.1 = (bf16[4,128,128]{2,1,0:T(8,128)(2,1)S(1)}, bf16[4,128,128]{2,1,0:T(8,128)(2,1)}, u32[]{:S(2)}) copy-start(bf16[4,128,128]{2,1,0:T(8,128)(2,1)} %refs_2_.1) | copy-start | bytes 393220

commit v2 on v1

--- a/solution.py
+++ b/solution.py
@@ -18,7 +18,6 @@
 SLOTS = Q_DEV * NSEG
 LANES = 128
 META = 8
-LEAD = 2
 TWIST = 2 * 2 * TP
 ROOT = math.sqrt(0.5)
 COS1, SIN1 = math.cos(math.pi / 8), math.sin(math.pi / 8)
@@ -156,8 +155,10 @@
 
 def pack_kernel(owners, capacity, me_ref, owner_hbm, place_hbm, kern_hbm, len_hbm, pix_hbm, *rest):
     chips = owners // 2
-    first, later = rest[:chips], rest[chips : 2 * chips]
-    swap_first, swap_later, lead, ints, pix, wide, sems = rest[2 * chips :]
+    head = far_order(owners)[0] // 2
+    keep = [j for j in range(chips) if j != head]
+    first, later = dict(zip(keep, rest)), dict(zip(keep, rest[chips - 1 :]))
+    swap_first, swap_later, ahead, ints, pix, wide, sems = rest[2 * chips - 2 :]
     tiles = ints.shape[1]
     shots = pix.shape[0] // tiles
     first_rows, later_rows = capacity + META, (shots - 1) * capacity
@@ -204,29 +205,31 @@
         j = d // 2
         if d % 2:
             near, far, at, to = swap_first, swap_later, j * first_rows, j * later_rows
+        elif j == head:
+            near, far, at, to = ahead, ahead, 0, first_rows
         else:
             near, far, at, to = first[j], later[j], 0, 0
         near[at : at + capacity, :] = sent[:, :TP]
         near[at + capacity : at + first_rows, :] = tags[d]
         for s in range(1, shots):
             start = to + (s - 1) * capacity
-            out = far
-            if d == owners // 2 and s >= shots - LEAD:
-                out, start = lead, (s + LEAD - shots) * capacity
-            out[start : start + capacity, :] = sent[:, s * TP : (s + 1) * TP]
-
-
-def merge_kernel(chips, shared, *refs):
-    own, other, outs = refs[: chips - 1], refs[chips - 1], refs[chips:]
+            far[start : start + capacity, :] = sent[:, s * TP : (s + 1) * TP]
+
+
+def merge_kernel(chips, head, shared, *refs):
+    own, other, outs = list(refs[: chips - 2]), refs[chips - 2], refs[chips - 1 :]
     size = other.shape[0] // chips
     body = size - shared
     for j in range(1, chips):
-        block, start, out = own[j - 1], j * size, outs[j - 1]
-        first = block.shape[0] - shared
-        out[:first, :] = block[:first, :]
-        out[first : first + body, :] = other[start : start + body, :]
+        start, out = j * size, outs[j - 1]
+        if j == head:
+            out[...] = other[start : start + size, :]
+            continue
+        block = own.pop(0)
+        out[:body, :] = block[:body, :]
+        out[body : 2 * body, :] = other[start : start + body, :]
         if shared:
-            out[first + body :, :] = block[first:, :] + other[start + body : start + size, :]
+            out[2 * body :, :] = block[body:, :] + other[start + body : start + size, :]
 
 
 def interpolate(pixels, kern, weights_ref):
@@ -248,18 +251,16 @@
     ]
 
 
-def gather_kernel(owners, capacity, *refs):
+def gather_kernel(capacity, spots, *refs):
     weights_hbm, pick_ref, live_ref, kern_ref, cyc0_ref, mask_ref, weights_ref, sem = refs[-8:]
     copy = pltpu.make_async_copy(weights_hbm, weights_ref, sem)
     copy.start()
-    got, metas = [], []
-    for j in range(owners // 2):
-        for core in range(2):
-            ref = refs[core] if j == 0 else refs[j + 1]
-            start = core * capacity if j else 0
-            tags = ref[ref.shape[0] - META :, :] if j else ref[capacity : capacity + META, :]
-            got.append(ref.at[pl.ds(start, capacity), :])
-            metas.append(tags.astype(F32)[4 * core : 4 * core + 4])
+    owners = len(spots)
+    got = [refs[i].at[pl.ds(start, capacity), :] for i, start, _ in spots]
+    metas = [
+        refs[i][row : row + META, :].astype(F32)[4 * (b % 2) : 4 * (b % 2) + 4]
+        for b, (i, _, row) in enumerate(spots)
+    ]
     group = math.gcd(owners, 4)
     for base in range(0, owners, group):
         tags = jnp.concatenate([m[1:3] for m in metas[base : base + group]], axis=0)
@@ -300,20 +301,6 @@
         scale_ref[m * Q_DEV : (m + 1) * Q_DEV, :] = (2.0 / ANG) / whole
 
 
-def late_blocks(far, capacity, shots, lead=None):
-    blocks = []
-    for ref in far:
-        for core in range(2):
-            start = core * (ref.shape[0] - shots * capacity)
-            held = shots if lead is None or blocks else shots - LEAD
-            block = [ref.at[pl.ds(start + s * capacity, capacity), :] for s in range(held)]
-            block += [
-                lead.at[pl.ds(s * capacity, capacity), :] for s in range(shots - held)
-            ]
-            blocks.append(block)
-    return blocks
-
-
 def late_cycles(blocks, live_ref, kern_ref, pick_ref, weights_ref, first):
     count = sum(ref.shape[0] for ref in blocks[0])
     capacity = count // len(blocks[0])
@@ -328,23 +315,30 @@
     return scatter(pick_ref[:, rows], values)
 
 
-def partial_kernel(capacity, shots, own, other, *refs):
-    (weights_ref, pick_ref, live_ref, kern_ref, next_ref, table_ref, part_ref, spec_ref) = refs[-8:]
-    blocks = [
-        [ref.at[pl.ds(s * capacity, capacity), :] for s in range(shots)] for ref in (own, other)
-    ]
-    blocks += late_blocks(refs[:-8], capacity, shots)
+def late_blocks(refs, capacity, shots, spots):
+    return [
+        [refs[i].at[pl.ds(start + s * capacity, capacity), :] for s in range(shots)]
+        for i, start in spots
+    ]
+
+
+def partial_kernel(capacity, shots, spots, *refs):
+    weights_ref, pick_ref, live_ref, kern_ref, part_ref = refs[-5:]
+    blocks = late_blocks(refs, capacity, shots, spots)
     cycles = late_cycles(blocks, live_ref, kern_ref, pick_ref, weights_ref, 0)
     for s, cycle in enumerate(cycles):
         part_ref[:, s * TP : (s + 1) * TP] = cycle
+
+
+def after_kernel(next_ref, table_ref, spec_ref):
     spec_ref[...] = spectrum([next_ref[...]], table_ref)
 
 
-def correlate_kernel(capacity, lead, *refs):
+def correlate_kernel(capacity, spots, *refs):
     (weights_ref, pick_ref, live_ref, kern_ref, part_ref, spec_ref, next_ref, scale_ref, table_ref,
      out_hbm, out, sems) = refs[-12:]
     shots = out.shape[0]
-    blocks = late_blocks(refs[:-12], capacity, shots - 1, lead)
+    blocks = late_blocks(refs, capacity, shots - 1, spots)
     first = live_ref.shape[0] - capacity * len(blocks)
     cycles = late_cycles(blocks, live_ref, kern_ref, pick_ref, weights_ref, first)
     cycles = [c + part_ref[:, s * TP : (s + 1) * TP] for s, c in enumerate(cycles)]
@@ -396,21 +390,27 @@
 
 
 def exchange(own, swap, owners, shared):
-    chips = owners // 2
+    chips, order = owners // 2, far_order(owners)
+    head = order[0] // 2
     other = cross(swap, 1, owners)
-    size = swap.shape[0] // chips - shared
+    size = swap.shape[0] // chips
     merged = call(
-        lambda *refs: merge_kernel(chips, shared, *refs),
-        [jax.ShapeDtypeStruct((block.shape[0] + size, TP), BF16) for block in own[1:]],
-        [*own[1:], other],
-    )
-    far = {d: cross(merged[d // 2 - 1], d, owners) for d in far_order(owners)}
-    return own[0], other, [far[d] for d in range(2, owners, 2)]
+        lambda *refs: merge_kernel(chips, head, shared, *refs),
+        [
+            jax.ShapeDtypeStruct((size if j == head else 2 * size - shared, TP), BF16)
+            for j in range(1, chips)
+        ],
+        [*(own[j] for j in range(1, chips) if j != head), other],
+    )
+    return other, {d: cross(merged[d // 2 - 1], d, owners) for d in order}
 
 
 def program(intensities, tile_owner, tile_place, tile_kernel, mask_len, interp_weights):
     owners = lax.axis_size("blk")
     chips = owners // 2
+    order, tail = far_order(owners), owners // 2
+    head = order[0]
+    keep = [j for j in range(chips) if 2 * j != head]
     ring = lax.axis_size("shot")
     tiles, shots, _ = intensities.shape
     capacity = -(-(3 * tiles // owners) // 16) * 16
@@ -419,14 +419,11 @@
     me = lax.axis_index("blk").astype(jnp.int32).reshape(1)
     sent = call(
         lambda *refs: pack_kernel(owners, capacity, *refs),
-        [jax.ShapeDtypeStruct((capacity + META, TP), BF16)] * chips
-        + [
-            jax.ShapeDtypeStruct(((shots - 1 - LEAD * (4 * j == owners)) * capacity, TP), BF16)
-            for j in range(chips)
-        ]
+        [jax.ShapeDtypeStruct((capacity + META, TP), BF16)] * (chips - 1)
+        + [jax.ShapeDtypeStruct(((shots - 1) * capacity, TP), BF16)] * (chips - 1)
         + [jax.ShapeDtypeStruct((chips * (capacity + META), TP), BF16)]
         + [jax.ShapeDtypeStruct((chips * (shots - 1) * capacity, TP), BF16)]
-        + [jax.ShapeDtypeStruct((LEAD * capacity, TP), BF16)],
+        + [jax.ShapeDtypeStruct((shots * capacity + META, TP), BF16)],
         [
             me,
             *(
@@ -448,14 +445,23 @@
             pltpu.SemaphoreType.DMA((5,)),
         ],
     )
-    lead = cross(sent[-1], owners // 2, owners)
-    own, other, far = exchange(sent[:chips], sent[2 * chips], owners, META)
-    last = chips // 2 - 1
-    early = [own, other, *far[:last], *far[last + 1 :], far[last]]
-    own, other, far = exchange(sent[chips : 2 * chips], sent[2 * chips + 1], owners, 0)
-    near, far = far[:last] + far[last + 1 :], far[last : last + 1]
+    first, later = dict(zip(keep, sent)), dict(zip(keep, sent[chips - 1 :]))
+    swap_first, swap_later, ahead = sent[-3:]
+    ahead = cross(ahead, head, owners)
+    other_first, far_first = exchange(first, swap_first, owners, META)
+    other_later, far_later = exchange(later, swap_later, owners, 0)
+    distant = [d for d in order if d not in (head, tail)] + [tail]
+    early = [first[0], other_first, ahead, far_first[head]] + [far_first[d] for d in distant]
+    early_spots = [(i, 0, capacity) for i in range(4)]
+    early_spots += [
+        (4 + i, core * capacity, 2 * capacity) for i in range(len(distant)) for core in range(2)
+    ]
+    near = [later[0], other_later, ahead, far_later[head]] + [far_later[d] for d in distant[:-1]]
+    near_spots = [(0, 0), (1, 0), (2, capacity + META), (3, 0)]
+    both = [(0, 0), (0, (shots - 1) * capacity)]
+    near_spots += [(4 + i, start) for i in range(len(distant) - 1) for _, start in both]
     pick, live, kern, cyc0, mask = call(
-        lambda *refs: gather_kernel(owners, capacity, *refs),
+        lambda *refs: gather_kernel(capacity, early_spots, *refs),
         [
             jax.ShapeDtypeStruct((SLOTS, rows), BF16),
             jax.ShapeDtypeStruct((rows, TP), BF16),
@@ -478,19 +484,19 @@
         [cyc0, mask, table],
         flops=10**9,
     )
-    part, after = call(
-        lambda *refs: partial_kernel(capacity, shots - 1, *refs),
-        [
-            jax.ShapeDtypeStruct((SLOTS, (shots - 1) * TP), F32),
-            jax.ShapeDtypeStruct((HALF * Q_DEV, 2 * TP), F32),
-        ],
-        [own, other, *near, interp_weights, pick, live, kern, after, table],
+    part = call(
+        lambda *refs: partial_kernel(capacity, shots - 1, near_spots, *refs),
+        jax.ShapeDtypeStruct((SLOTS, (shots - 1) * TP), F32),
+        [*near, interp_weights, pick, live, kern],
         flops=10**9,
     )
+    after = call(
+        after_kernel, jax.ShapeDtypeStruct((HALF * Q_DEV, 2 * TP), F32), [after, table], flops=10**8
+    )
     return call(
-        lambda *refs: correlate_kernel(capacity, *refs),
+        lambda *refs: correlate_kernel(capacity, both, *refs),
         jax.ShapeDtypeStruct((shots, Q_DEV, ANG), F32),
-        [lead, *far, interp_weights, pick, live, kern, part, spec, after, scale, table],
+        [far_later[tail], interp_weights, pick, live, kern, part, spec, after, scale, table],
         out_specs=HBM,
         scratch=[
             pltpu.VMEM((shots, Q_DEV, ANG), F32),

time: 29.9 us -> 32.9 us (1.10)
  waiting for transfers between devices: 6.38 us -> 10 us
  starting transfers between devices: 16 us -> 15.3 us
  Pallas kernels: 7.03 us -> 7.36 us
    ppermute x9, waiting for transfers between devices: 6.38 us -> 10 us  [cross(): return lax.ppermute(block, 'blk', [(i, i ^ d) for i in range(owners)])]
    ppermute x9, starting transfers between devices: 13.5 us -> 12.8 us  [cross(): return lax.ppermute(block, 'blk', [(i, i ^ d) for i in range(owners)])]
    pallas_call x7 -> x8, Pallas kernels: 7.03 us -> 7.36 us  [call(): pl.pallas_call(body, out_shape=outs, in_specs=in_specs or [VMEM] * len(op...]
  transfers between devices with their start and end apart: 10 -> 10, of which waited for: 4 -> 3; matrix products, arithmetic and copies ran while one was open for 0% -> 0% of each run, Pallas kernels for 11% -> 11%
where the time goes in v2:
time: 32.9 us; the launch traced here: 32.8 us
  starting transfers between devices  15.3 us (47%)
  waiting for transfers between devices  10 us (30%)
  Pallas kernels  7.36 us (22%)
    ppermute x9, starting transfers between devices, cross(): return lax.ppermute(block, 'blk', [(i, i ^ d) for i in range(owners)])  12.8 us
    ppermute x9, waiting for transfers between devices, cross(): return lax.ppermute(block, 'blk', [(i, i ^ d) for i in range(owners)])  10 us
    pallas_call x8, Pallas kernels, call(): pl.pallas_call(body, out_shape=outs, in_specs=in_specs or [VMEM] * len(op...  7.36 us
    ppermute x1, starting transfers between devices, program(): lax.ppermute(cyc0, 'shot', [((i + 1) % ring, i) for i in range(ring)])  2.5 us
  transfers between devices with their start and end apart: 10, of which 3 were waited for; matrix products, arithmetic and copies ran while one was open for 0% of the time, Pallas kernels for 11%

profile of v2, /device:TPU:0, one launch (start us, length us, event | category | flops | bytes accessed | tf_op | source)
XLA Modules:
  0.0 32.8 jit_solution(13449168431737187049)
XLA Ops:
  0.0 1.6 %shard_map.73 = (bf16[104,128]{1,0:T(8,128)(2,1)S(1)}, bf16[104,128]{1,0:T(8,128)(2,1)S(1)}, bf16[104,128]{1,0:T(8,128)(2,1)S(1)}, bf16[288,128]{1,0:T(8,128)(2,...) custom-call(s32[1]{0:T(128)} %bitcast.refs_0_, ...), custom_call_target="tpu_custom_call" | custom-call | bytes 1048576 | tf_op jit(solution)/shard_map/pallas_call | solution.py:373
  1.7 0.6 %collective-permute-start = (bf16[1152,128]{1,0:T(8,128)(2,1)S(1)}, bf16[1152,128]{1,0:T(8,128)(2,1)S(1)}, u32[]{:S(2)}, u32[]{:S(2)}) collective-permute-start(bf16[1152,128]{1,0:T(8,128)(2,1)S(1)} %get-tuple-element.29), channel_id=1, source_target_pairs={{0,1},{1,0},{2,3},{3,2},{4,5},{5,4},{6,7},{7,6},{8,9},{9,8},{10,11... | collective-permute-start | bytes 884744 | tf_op jit(solution)/shard_map/ppermute | solution.py:389
  2.2 0.1 collective-permute-start.2
  2.3 5.0 %collective-permute-start.3 = (bf16[392,128]{1,0:T(8,128)(2,1)S(1)}, bf16[392,128]{1,0:T(8,128)(2,1)S(1)}, u32[]{:S(2)}, u32[]{:S(2)}) collective-permute-start(bf16[392,128]{1,0:T(8,128)(2,1)S(1)} %get-tuple-element.33), channel_id=1, source_target_pairs={{0,6},{1,7},{2,4},{3,5},{4,2},{5,3},{6,0},{7,1},{8,14},{9,15},{10,... | collective-permute-start | bytes 301064 | tf_op jit(solution)/shard_map/ppermute | solution.py:389
  7.3 0.0 collective-permute-done.2.refs_2_.refs_1_
  7.3 0.1 collective-permute-start.5
  7.4 1.8 %collective-permute-start.6 = (bf16[200,128]{1,0:T(8,128)(2,1)S(1)}, bf16[200,128]{1,0:T(8,128)(2,1)S(1)}, u32[]{:S(2)}, u32[]{:S(2)}) collective-permute-start(bf16[200,128]{1,0:T(8,128)(2,1)S(1)} %get-tuple-element.38), channel_id=1, source_target_pairs={{0,4},{1,5},{2,6},{3,7},{4,0},{5,1},{6,2},{7,3},{8,12},{9,13},{10,... | collective-permute-start | bytes 153608 | tf_op jit(solution)/shard_map/ppermute | solution.py:389
  9.2 2.6 %collective-permute-start.4 = (bf16[104,128]{1,0:T(8,128)(2,1)S(1)}, bf16[104,128]{1,0:T(8,128)(2,1)S(1)}, u32[]{:S(2)}, u32[]{:S(2)}) collective-permute-start(bf16[104,128]{1,0:T(8,128)(2,1)S(1)} %get-tuple-element.36), channel_id=1, source_target_pairs={{0,6},{1,7},{2,4},{3,5},{4,2},{5,3},{6,0},{7,1},{8,14},{9,15},{10,... | collective-permute-start | bytes 79880 | tf_op jit(solution)/shard_map/ppermute | solution.py:389
  11.8 0.0 collective-permute-done.refs_2_.refs_1_
  11.8 0.1 collective-permute-start.8
  11.9 0.0 collective-permute-done.3.refs_2_
  11.9 3.2 %collective-permute-done.4.refs_3_ = bf16[104,128]{1,0:T(8,128)(2,1)S(1)} collective-permute-done((bf16[104,128]{1,0:T(8,128)(2,1)S(1)}, bf16[104,128]{1,0:T(8,128)(2,1)S(1)}, u32[]{:S(2)}, u32[]{:S(2)}) %collective-permute-start.4) | collective-permute-done | bytes 26656 | tf_op jit(solution)/shard_map/ppermute | solution.py:389
  15.1 0.0 collective-permute-done.5.refs_4_
  15.1 0.0 collective-permute-done.6.refs_5_
  15.1 0.0 copy-start
  15.1 1.8 %shard_map.76 = (bf16[256,768]{1,0:T(8,128)(2,1)S(1)}, bf16[768,128]{1,0:T(8,128)(2,1)S(1)}, f32[768,128]{1,0:T(8,128)S(1)}, f32[256,128]{1,0:T(8,128)S(1)}, f32[256,128]{1,0:T(8,128)S(1)}) custom-call(bf16[104,128]{1,0:T(8,128)(2,1)S(1)} %get-tuple-element.31.refs_0_, bf16[416,128]{1,0:T(8,128)(2,1)S(1)} %collective-permute-done.2.refs_2_.refs_1_, ...), custom_call_target="tpu_custom_call" | custom-call | flops 2000000000 | bytes 1048576 | tf_op jit(solution)/shard_map/pallas_call | solution.py:373
  17.0 2.5 %collective-permute-start.9 = (f32[256,128]{1,0:T(8,128)S(1)}, f32[256,128]{1,0:T(8,128)S(1)}, u32[]{:S(2)}, u32[]{:S(2)}) collective-permute-start(f32[256,128]{1,0:T(8,128)S(1)} %get-tuple-element.45.cyc0_ref), channel_id=1, source_target_pairs={{8,0},{16,8},{24,16},{0,24},{9,1},{17,9},{25,17},{1,25},{10,2},{18... | collective-permute-start | bytes 393224 | tf_op jit(solution)/shard_map/ppermute | solution.py:477
  19.5 2.6 %collective-permute-start.7 = (bf16[288,128]{1,0:T(8,128)(2,1)S(1)}, bf16[288,128]{1,0:T(8,128)(2,1)S(1)}, u32[]{:S(2)}, u32[]{:S(2)}) collective-permute-start(bf16[288,128]{1,0:T(8,128)(2,1)S(1)} %get-tuple-element.43), channel_id=1, source_target_pairs={{0,6},{1,7},{2,4},{3,5},{4,2},{5,3},{6,0},{7,1},{8,14},{9,15},{10,... | collective-permute-start | bytes 221192 | tf_op jit(solution)/shard_map/ppermute | solution.py:389
  22.1 0.0 collective-permute-start.1
  22.1 0.0 copy-done
  22.1 0.6 %shard_map.78 = (f32[144,256]{1,0:T(8,128)S(1)}, f32[256,128]{1,0:T(8,128)S(1)}) custom-call(f32[256,128]{1,0:T(8,128)S(1)} %get-tuple-element.45.cyc0_ref, f32[256,128]{1,0:T(8,128)S(1)} %get-tuple-element.46.mask_ref, bf16[560,256]{1,0:T(8,128)(2,1)S(1)} %copy-done), custom_call_target="tpu_custom_call" | custom-call | flops 1000000000 | bytes 1048576 | tf_op jit(solution)/shard_map/pallas_call | solution.py:373
  22.7 0.0 copy-start.1
  22.7 0.0 collective-permute-done.9.next_ref
  22.7 0.2 shard_map.79.refs_7_
  23.0 3.1 %collective-permute-done.7.refs_3_ = bf16[288,128]{1,0:T(8,128)(2,1)S(1)} collective-permute-done((bf16[288,128]{1,0:T(8,128)(2,1)S(1)}, bf16[288,128]{1,0:T(8,128)(2,1)S(1)}, u32[]{:S(2)}, u32[]{:S(2)}) %collective-permute-start.7) | collective-permute-done | bytes 73760 | tf_op jit(solution)/shard_map/ppermute | solution.py:389
  26.1 0.0 collective-permute-done.8.refs_4_
  26.1 0.0 copy-done.1
  26.1 1.0 %shard_map.77.refs_5_ = f32[256,384]{1,0:T(8,128)S(1)} custom-call(bf16[288,128]{1,0:T(8,128)(2,1)S(1)} %get-tuple-element.42.refs_0_, bf16[1152,128]{1,0:T(8,128)(2,1)S(1)} %collective-permute-done.refs_2_.refs_1_, bf16[392,128]{1,0:T(8,128)(2,1)S(1)} %collective-permute-done.3.refs_2_, bf16[288,128]{1,0:T(8,128)(2,1)S(1)} %collective-permute-done.7.refs_3_, ...), custom_call_target="tpu_custom_call" | custom-call | flops 1000000000 | bytes 1048576 | tf_op jit(solution)/shard_map/pallas_call | solution.py:373
  27.0 3.7 %collective-permute-done.1.refs_0_ = bf16[576,128]{1,0:T(8,128)(2,1)S(1)} collective-permute-done((bf16[576,128]{1,0:T(8,128)(2,1)S(1)}, bf16[576,128]{1,0:T(8,128)(2,1)S(1)}, u32[]{:S(2)}, u32[]{:S(2)}) %collective-permute-start.1) | collective-permute-done | bytes 147488 | tf_op jit(solution)/shard_map/ppermute | solution.py:389
  30.8 2.0 %shard_map.80 = f32[4,16,2048]{2,1,0:T(8,128)} custom-call(bf16[576,128]{1,0:T(8,128)(2,1)S(1)} %collective-permute-done.1.refs_0_, bf16[4,128,128]{2,1,0:T(8,128)(2,1)S(1)} %copy-done.1, bf16[256,768]{1,0:T(8,128)(2,1)S(1)} %get-tuple-element.39.refs_6_.refs_2_, bf16[768,128]{1,0:T(8,128)(2,1)S(1)} %get-tuple-element.40.refs_7_.refs_3_, ...), custom_call_target="tpu_custom_call" | custom-call | bytes 1048576 | tf_op jit(solution)/shard_map/pallas_call | solution.py:373
  (2 shorter events, 0.0 us)
Async XLA Ops:
  1.7 10.1 %collective-permute-start = (bf16[1152,128]{1,0:T(8,128)(2,1)S(1)}, bf16[1152,128]{1,0:T(8,128)(2,1)S(1)}, u32[]{:S(2)}, u32[]{:S(2)}) collective-permute-start(bf16[1152,128]{1,0:T(8,128)(2,1)S(1)} %get-tuple-element.29), channel_id=1, source_target_pairs={{0,1},{1,0},{2,3},{3,2},{4,5},{5,4},{6,7},{7,6},{8,9},{9,8},{10,11... | collective-permute-start | bytes 884744 | tf_op jit(solution)/shard_map/ppermute | solution.py:389
  2.2 5.1 %collective-permute-start.2 = (bf16[416,128]{1,0:T(8,128)(2,1)S(1)}, bf16[416,128]{1,0:T(8,128)(2,1)S(1)}, u32[]{:S(2)}, u32[]{:S(2)}) collective-permute-start(bf16[416,128]{1,0:T(8,128)(2,1)S(1)} %get-tuple-element.32), channel_id=1, source_target_pairs={{0,1},{1,0},{2,3},{3,2},{4,5},{5,4},{6,7},{7,6},{8,9},{9,8},{10,11... | collective-permute-start | bytes 319496 | tf_op jit(solution)/shard_map/ppermute | solution.py:389
  2.3 9.6 %collective-permute-start.3 = (bf16[392,128]{1,0:T(8,128)(2,1)S(1)}, bf16[392,128]{1,0:T(8,128)(2,1)S(1)}, u32[]{:S(2)}, u32[]{:S(2)}) collective-permute-start(bf16[392,128]{1,0:T(8,128)(2,1)S(1)} %get-tuple-element.33), channel_id=1, source_target_pairs={{0,6},{1,7},{2,4},{3,5},{4,2},{5,3},{6,0},{7,1},{8,14},{9,15},{10,... | collective-permute-start | bytes 301064 | tf_op jit(solution)/shard_map/ppermute | solution.py:389
  7.3 7.8 %collective-permute-start.5 = (bf16[200,128]{1,0:T(8,128)(2,1)S(1)}, bf16[200,128]{1,0:T(8,128)(2,1)S(1)}, u32[]{:S(2)}, u32[]{:S(2)}) collective-permute-start(bf16[200,128]{1,0:T(8,128)(2,1)S(1)} %get-tuple-element.37), channel_id=1, source_target_pairs={{0,2},{1,3},{2,0},{3,1},{4,6},{5,7},{6,4},{7,5},{8,10},{9,11},{10,... | collective-permute-start | bytes 153608 | tf_op jit(solution)/shard_map/ppermute | solution.py:389
  7.4 7.7 %collective-permute-start.6 = (bf16[200,128]{1,0:T(8,128)(2,1)S(1)}, bf16[200,128]{1,0:T(8,128)(2,1)S(1)}, u32[]{:S(2)}, u32[]{:S(2)}) collective-permute-start(bf16[200,128]{1,0:T(8,128)(2,1)S(1)} %get-tuple-element.38), channel_id=1, source_target_pairs={{0,4},{1,5},{2,6},{3,7},{4,0},{5,1},{6,2},{7,3},{8,12},{9,13},{10,... | collective-permute-start | bytes 153608 | tf_op jit(solution)/shard_map/ppermute | solution.py:389
  9.2 5.9 %collective-permute-start.4 = (bf16[104,128]{1,0:T(8,128)(2,1)S(1)}, bf16[104,128]{1,0:T(8,128)(2,1)S(1)}, u32[]{:S(2)}, u32[]{:S(2)}) collective-permute-start(bf16[104,128]{1,0:T(8,128)(2,1)S(1)} %get-tuple-element.36), channel_id=1, source_target_pairs={{0,6},{1,7},{2,4},{3,5},{4,2},{5,3},{6,0},{7,1},{8,14},{9,15},{10,... | collective-permute-start | bytes 79880 | tf_op jit(solution)/shard_map/ppermute | solution.py:389
  11.8 14.3 %collective-permute-start.8 = (bf16[576,128]{1,0:T(8,128)(2,1)S(1)}, bf16[576,128]{1,0:T(8,128)(2,1)S(1)}, u32[]{:S(2)}, u32[]{:S(2)}) collective-permute-start(bf16[576,128]{1,0:T(8,128)(2,1)S(1)} %get-tuple-element.44), channel_id=1, source_target_pairs={{0,2},{1,3},{2,0},{3,1},{4,6},{5,7},{6,4},{7,5},{8,10},{9,11},{10,... | collective-permute-start | bytes 442376 | tf_op jit(solution)/shard_map/ppermute | solution.py:389
  15.1 7.0 %copy-start = (bf16[560,256]{1,0:T(8,128)(2,1)S(1)}, bf16[560,256]{1,0:T(8,128)(2,1)}, u32[]{:S(2)}) copy-start(bf16[560,256]{1,0:T(8,128)(2,1)} %constant.6.clone.table_ref.refs_9_) | copy-start | bytes 860164
  17.0 5.8 %collective-permute-start.9 = (f32[256,128]{1,0:T(8,128)S(1)}, f32[256,128]{1,0:T(8,128)S(1)}, u32[]{:S(2)}, u32[]{:S(2)}) collective-permute-start(f32[256,128]{1,0:T(8,128)S(1)} %get-tuple-element.45.cyc0_ref), channel_id=1, source_target_pairs={{8,0},{16,8},{24,16},{0,24},{9,1},{17,9},{25,17},{1,25},{10,2},{18... | collective-permute-start | bytes 393224 | tf_op jit(solution)/shard_map/ppermute | solution.py:477
  19.5 6.6 %collective-permute-start.7 = (bf16[288,128]{1,0:T(8,128)(2,1)S(1)}, bf16[288,128]{1,0:T(8,128)(2,1)S(1)}, u32[]{:S(2)}, u32[]{:S(2)}) collective-permute-start(bf16[288,128]{1,0:T(8,128)(2,1)S(1)} %get-tuple-element.43), channel_id=1, source_target_pairs={{0,6},{1,7},{2,4},{3,5},{4,2},{5,3},{6,0},{7,1},{8,14},{9,15},{10,... | collective-permute-start | bytes 221192 | tf_op jit(solution)/shard_map/ppermute | solution.py:389
  22.1 8.7 %collective-permute-start.1 = (bf16[576,128]{1,0:T(8,128)(2,1)S(1)}, bf16[576,128]{1,0:T(8,128)(2,1)S(1)}, u32[]{:S(2)}, u32[]{:S(2)}) collective-permute-start(bf16[576,128]{1,0:T(8,128)(2,1)S(1)} %get-tuple-element.30), channel_id=1, source_target_pairs={{0,4},{1,5},{2,6},{3,7},{4,0},{5,1},{6,2},{7,3},{8,12},{9,13},{10,... | collective-permute-start | bytes 442376 | tf_op jit(solution)/shard_map/ppermute | solution.py:389
  22.7 3.3 %copy-start.1 = (bf16[4,128,128]{2,1,0:T(8,128)(2,1)S(1)}, bf16[4,128,128]{2,1,0:T(8,128)(2,1)}, u32[]{:S(2)}) copy-start(bf16[4,128,128]{2,1,0:T(8,128)(2,1)} %refs_1_.1) | copy-start | bytes 393220
